TPU v7x, 32 devices: a whole 2x2x4 slice. The times are simulated.
32 devices in a mesh: sec: 4 (over y, x), strip: 8 (over z, core).
Axes of the slice: x: 2, y: 2, z: 4, core: 2. Of those that a mesh axis runs over, the one named last changes fastest.
Arguments:
- features: bfloat16 [4, 96, 128, 128], P('sec', 'strip'), may hold values from -6 to 6
- offsets: int32 [4], replicated, may hold values from -2 to 2
- state: float32 [2, 4, 96, 128], P(None, 'sec', 'strip'), may hold values from -6 to 6
- w_first: bfloat16 [3, 3, 162, 128], replicated, may hold values from -0.15625 to 0.15625
- b_first: float32 [128], replicated, may hold values from -3 to 3
- w_second: bfloat16 [3, 3, 128, 128], replicated, may hold values from -0.1875 to 0.1875
- b_second: float32 [128], replicated, may hold values from -3 to 3
- w_third: bfloat16 [3, 3, 128, 2], replicated, may hold values from -0.1875 to 0.1875
Outputs:
- updated: float32 [2, 4, 96, 128], P(None, 'sec', 'strip')
Inputs may be any that keep to these rules, and one draw needn't show every extreme that they name: offsets[s] is the integer row offset of section s+1 against section s; the last entry is not used.
All inputs are finite; a program needn't handle non-finite values.
Results may differ from a plain program's by a relative error of at most 0.0029.
Values may be sent and summed in bfloat16 or wider, within the bound.
A program may use at most 64 MiB of HBM per device.

v0:
```python
import functools

import jax
import jax.numpy as jnp
from jax import lax
from jax.experimental import pallas as pl
from jax.experimental.pallas import tpu as pltpu
from jax.sharding import PartitionSpec as P

SIDE = 9
STEP = 3
PIECE = STEP
TAPS = 9
VMEM = pl.BlockSpec(memory_space=pltpu.VMEM)
HBM = pl.BlockSpec(memory_space=pltpu.HBM)
SMEM = pl.BlockSpec(memory_space=pltpu.SMEM)


def group_of(rows):
    return max(g for g in range(1, 8) if rows % g == 0)


def exchange(secs, strips, feat, mine, near, far, send_sem, recv_sem, loads, prepare, turn, relate):
    rows = feat.shape[1]
    count = rows // PIECE
    sec, strip = lax.axis_index("sec"), lax.axis_index("strip")
    odd = lax.rem(sec, 2)
    partner = sec + 1 - 2 * odd
    relay_to, relay_from = sec + 2 - 4 * odd, sec - 2 + 4 * odd
    has_to = (relay_to >= 0) & (relay_to < secs)
    has_from = (relay_from >= 0) & (relay_from < secs)
    has_low, has_high = strip > 0, strip < strips - 1

    barrier = pltpu.get_barrier_semaphore()
    greeted = (
        (None, partner, strip),
        (has_to, relay_to, strip),
        (has_from, relay_from, strip),
        (has_low, sec, strip - 1),
        (has_high, sec, strip + 1),
    )

    def when(cond, act):
        if cond is None:
            act()
        else:
            pl.when(cond)(act)

    for cond, a, b in greeted:
        when(cond, lambda a=a, b=b: pl.semaphore_signal(barrier, inc=1, device_id=(a, b), device_id_type=pl.DeviceIdType.MESH))

    for load in loads:
        load.start()
    pl.semaphore_wait(barrier, 1 + sum(cond.astype(jnp.int32) for cond, _, _ in greeted[1:]))

    waits = []
    number = [0]

    def copy(src, dst, a, b, sends, gets):
        at = number[0]
        number[0] += 1
        made = pltpu.make_async_remote_copy(
            src_ref=src, dst_ref=dst, send_sem=send_sem.at[at], recv_sem=recv_sem.at[at],
            device_id=(a, b), device_id_type=pl.DeviceIdType.MESH,
        )
        when(sends, made.start)
        waits.append((sends, made.wait_send))
        return lambda: when(gets, made.wait_recv)

    def both(x, y):
        return y if x is None else x & y

    def down(slot, q, known):
        return copy(
            slot.at[pl.ds(SIDE + PIECE * q, PIECE)], slot.at[pl.ds(SIDE + rows + PIECE * q, PIECE)],
            sec, strip - 1, both(known, has_low), both(known, has_high),
        )

    def up(slot, q, known):
        return copy(
            slot.at[pl.ds(SIDE + PIECE * q, PIECE)], slot.at[pl.ds(SIDE + PIECE * q - rows, PIECE)],
            sec, strip + 1, both(known, has_high), both(known, has_low),
        )

    order = list(range(count))
    direct = [
        copy(feat.at[0, pl.ds(PIECE * q, PIECE)], near.at[pl.ds(SIDE + PIECE * q, PIECE)], partner, strip, None, None)
        for q in order
    ]
    last = []
    last.append(copy(feat.at[0, pl.ds(0, STEP)], mine.at[pl.ds(STEP + rows, STEP)], sec, strip - 1, has_low, has_high))
    last.append(copy(feat.at[0, pl.ds(rows - STEP, STEP)], mine.at[pl.ds(0, STEP)], sec, strip + 1, has_high, has_low))

    zero = jnp.zeros((SIDE,) + near.shape[1:], near.dtype)

    @pl.when(jnp.logical_not(has_from))
    def _():
        far[...] = jnp.zeros(far.shape, far.dtype)

    @pl.when(jnp.logical_not(has_low))
    def _():
        near[0:SIDE] = zero
        far[0:SIDE] = zero
        mine[0:STEP] = zero[:STEP]

    @pl.when(jnp.logical_not(has_high))
    def _():
        near[SIDE + rows:] = zero
        far[SIDE + rows:] = zero
        mine[STEP + rows:] = zero[:STEP]

    relayed = []
    ends = ([], [])

    def sides(slot, q, known, found):
        if PIECE * q < SIDE:
            found.append(down(slot, q, known))
        if PIECE * q >= rows - SIDE:
            found.append(up(slot, q, known))

    for q in order + [count]:
        if q < count:
            direct[q]()
            relayed.append(copy(
                near.at[pl.ds(SIDE + PIECE * q, PIECE)], far.at[pl.ds(SIDE + PIECE * q, PIECE)],
                relay_to, strip, has_to, has_from,
            ))
            sides(near, q, None, ends[0])
        if q >= 1:
            relayed[q - 1]()
            sides(far, q - 1, has_from, ends[1])
        if q == count // 4:
            prepare()
        if q == count // 2:
            for wait in last:
                wait()
            turn()
    for wide, found, slot in zip((near, far), ends, (1 - odd, odd)):
        for wait in found:
            wait()
        relate(wide, slot)
    for cond, wait in waits:
        when(cond, wait)


def convolve(sources, weight, bias, target):
    rows, cols, width = target.shape
    depth = sources[0].shape[2]
    group = group_of(rows)
    at_col = lax.broadcasted_iota(jnp.int32, (cols, width), 0)

    def step(g, carry):
        base = g * group
        taken = jnp.concatenate(
            [s[pl.ds(base + d, group)].reshape(group * cols, depth) for d in range(3) for s in sources], axis=1
        )
        sums = jnp.dot(taken, weight[...], preferred_element_type=jnp.float32)
        for i in range(group):
            one = sums[i * cols:(i + 1) * cols]
            before = jnp.where(at_col == 0, 0.0, pltpu.roll(one[:, :width], 1, 0))
            after = jnp.where(at_col == cols - 1, 0.0, pltpu.roll(one[:, 2 * width:], cols - 1, 0))
            total = one[:, width:2 * width] + before + after + bias[...]
            target[base + i] = jnp.maximum(total, 0.0).astype(target.dtype)
        return carry

    lax.fori_loop(0, rows // group, step, 0)


def skewed(block, shift):
    rows, cols = block.shape
    pieces = []
    start = 0
    for top in range(0, rows, 8):
        if (shift + top) % cols + 7 > cols:
            if top > start:
                pieces.append(pltpu.roll(block[start:top], (shift + start) % cols, 1, stride=1, stride_axis=0))
            crossing = pltpu.roll(block[top:top + 8], (shift + top - 8) % cols, 1, stride=1, stride_axis=0)
            pieces.append(pltpu.roll(crossing, 8, 1))
            start = top + 8
    if start < rows:
        pieces.append(pltpu.roll(block[start:], (shift + start) % cols, 1, stride=1, stride_axis=0))
    return jnp.concatenate(pieces, axis=0)


def kernel(secs, strips, feat, offsets, w_one, b_one, w_two, b_two, w_three, out,
           mine, near, far, corr, hid_one, hid_two, held_one, held_two, wide_one, wide_two, thirds,
           send_sem, recv_sem, local_sem):
    rows, cols, chans = feat.shape[1:]
    hid = b_one.shape[1]
    planes = w_one.shape[2] // 2
    sec, strip = lax.axis_index("sec"), lax.axis_index("strip")
    loads = [
        pltpu.make_async_copy(feat.at[0], mine.at[pl.ds(STEP, rows)], local_sem.at[0]),
        pltpu.make_async_copy(w_one, held_one, local_sem.at[1]),
        pltpu.make_async_copy(w_two, held_two, local_sem.at[2]),
    ]

    def prepare():
        for d in range(3):
            thirds[8 * d:8 * d + 8] = jnp.zeros((8, hid), thirds.dtype)
            for e in range(3):
                thirds[8 * d + 4 - 2 * e:8 * d + 6 - 2 * e] = w_three[d, e].astype(thirds.dtype)
        for d in range(2 * 3):
            wide_one[d * cols + planes // 16 * 16:(d + 1) * cols] = jnp.zeros((cols - planes // 16 * 16, 3 * hid), wide_one.dtype)
        loads[1].wait()
        loads[2].wait()
        for d in range(3):
            for e in range(3):
                at = pl.ds((2 - e) * hid, hid)
                for j in range(2):
                    wide_one[pl.ds((2 * d + j) * cols, planes), at] = held_one[d, e, j * planes:(j + 1) * planes]
                wide_two[pl.ds(d * hid, hid), at] = held_two[d, e]
        loads[0].wait()

    scale = chans ** (-0.5)
    lane = lax.broadcasted_iota(jnp.int32, (cols, cols), 1)
    col = lax.broadcasted_iota(jnp.int32, (cols, cols), 0)
    flip = (lane + col == cols - 1).astype(mine.dtype)
    other = cols - 1 - col + lax.rem(lane, TAPS) - 4
    gain = jnp.where((other >= 0) & (other < cols) & (lane < planes), scale, 0.0)
    shifts = (
        jnp.where(sec > 0, -offsets[jnp.maximum(sec - 1, 0)], 0),
        jnp.where(sec < secs - 1, offsets[sec], 0),
    )

    def turn():
        def one(r, carry):
            mine[r] = jnp.dot(flip, mine[r], preferred_element_type=jnp.float32).astype(mine.dtype)
            return carry

        lax.fori_loop(0, rows + 6, one, 0)

    group = 6 if rows % 6 == 0 else 2

    def relate(wide, slot):
        shift = jnp.where(slot == 0, shifts[0], shifts[1])

        def step(g, carry):
            base = g * group
            here = mine[pl.ds(base, group)].reshape(group * cols, chans)
            products = {}
            for t in range(0, group + TAPS - 1, 2):
                low, high = max(0, t - TAPS + 1), min(group, t + 2)
                there = wide[pl.ds(base + 2 + shift + t, 2)].reshape(2 * cols, chans)
                tile = lax.dot_general(
                    here[low * cols:high * cols], there, (((1,), (1,)), ((), ())), preferred_element_type=jnp.float32
                )
                for i in range(low, high):
                    for u in range(2):
                        if 0 <= t + u - i < TAPS:
                            products[i, t + u - i] = tile[(i - low) * cols:(i - low + 1) * cols, u * cols:(u + 1) * cols]
            for i in range(group):
                found = skewed(products[i, 0], 5)
                for a in range(1, TAPS):
                    found = jnp.where(lane >= a * TAPS, skewed(products[i, a], a * TAPS + 5), found)
                corr[slot, base + i] = (found * gain).astype(corr.dtype)
            return carry

        lax.fori_loop(0, (rows + 6) // group, step, 0)

    exchange(secs, strips, feat, mine, near, far, send_sem, recv_sem, loads, prepare, turn, relate)

    convolve((corr.at[0], corr.at[1]), wide_one, b_one, hid_one)

    @pl.when(strip == 0)
    def _():
        hid_one[0:2] = jnp.zeros((2, cols, hid), hid_one.dtype)

    @pl.when(strip == strips - 1)
    def _():
        hid_one[rows + 2:] = jnp.zeros((2, cols, hid), hid_one.dtype)

    convolve((hid_one,), wide_two, b_two, hid_two)

    @pl.when(strip == 0)
    def _():
        hid_two[0:1] = jnp.zeros((1, cols, hid), hid_two.dtype)

    @pl.when(strip == strips - 1)
    def _():
        hid_two[rows + 1:] = jnp.zeros((1, cols, hid), hid_two.dtype)

    taps = lax.dot_general(
        thirds[...].astype(hid_two.dtype), hid_two[...].reshape((rows + 2) * cols, hid), (((1,), (1,)), ((), ())),
        preferred_element_type=jnp.float32,
    )
    at_lane = lax.broadcasted_iota(jnp.int32, (8, cols), 1)
    found = []
    for r in range(rows):
        total = sum(taps[8 * d:8 * d + 8, (r + d) * cols:(r + d + 1) * cols] for d in range(3))
        before = jnp.where(at_lane == 0, 0.0, pltpu.roll(total, 1, 1))
        after = jnp.where(at_lane == cols - 1, 0.0, pltpu.roll(total, cols - 1, 1))
        found.append(before[0:2] + total[2:4] + after[4:6])
    turned = jnp.dot(
        jnp.concatenate(found, axis=0), flip.astype(jnp.float32),
        preferred_element_type=jnp.float32, precision=lax.Precision.HIGHEST,
    )
    for r in range(rows):
        for p in range(2):
            out[p * rows + r] = turned[2 * r + p:2 * r + p + 1]


def body(secs, strips, features, offsets, state, w_first, b_first, w_second, b_second, w_third):
    _, rows, cols, chans = features.shape
    hid = w_first.shape[3]
    parts = w_third.shape[3]
    copies = 2 * (rows // PIECE) + 4 * (SIDE // PIECE) + 2
    bf16 = jnp.bfloat16
    delta = pl.pallas_call(
        functools.partial(kernel, secs, strips),
        out_shape=jax.ShapeDtypeStruct((parts * rows, 1, cols), jnp.float32),
        in_specs=[HBM, SMEM, HBM, VMEM, HBM, VMEM, VMEM],
        out_specs=VMEM,
        scratch_shapes=[
            pltpu.VMEM((rows + 6, cols, chans), bf16),
            pltpu.VMEM((rows + 2 * SIDE, cols, chans), bf16),
            pltpu.VMEM((rows + 2 * SIDE, cols, chans), bf16),
            pltpu.VMEM((2, rows + 6, cols, cols), bf16),
            pltpu.VMEM((rows + 4, cols, hid), bf16),
            pltpu.VMEM((rows + 2, cols, hid), bf16),
            pltpu.VMEM(w_first.shape, bf16),
            pltpu.VMEM(w_second.shape, bf16),
            pltpu.VMEM((6 * cols, 3 * hid), bf16),
            pltpu.VMEM((3 * hid, 3 * hid), bf16),
            pltpu.VMEM((24, hid), jnp.float32),
            pltpu.SemaphoreType.DMA((copies,)),
            pltpu.SemaphoreType.DMA((copies,)),
            pltpu.SemaphoreType.DMA((3,)),
        ],
        compiler_params=pltpu.CompilerParams(collective_id=0, has_side_effects=True, vmem_limit_bytes=56 << 20),
    )(
        features, offsets, w_first, b_first.reshape(1, hid), w_second, b_second.reshape(1, hid),
        jnp.transpose(w_third, (0, 1, 3, 2)),
    )
    return state + delta.reshape(state.shape)


def solution(mesh):
    secs, strips = mesh.shape["sec"], mesh.shape["strip"]
    in_specs = (
        P("sec", "strip", None, None),
        P(),
        P(None, "sec", "strip", None),
        P(),
        P(),
        P(),
        P(),
        P(),
    )
    out_specs = P(None, "sec", "strip", None)
    return jax.shard_map(functools.partial(body, secs, strips), mesh=mesh, in_specs=in_specs, out_specs=out_specs, check_vma=False)
```

profile of v0, /device:TPU:19, one launch (start us, length us, event | category | flops | bytes accessed | tf_op | source)
XLA Modules:
  0.0 32.7 jit_solution(5273156049440848343)
XLA Ops:
  0.0 0.0 copy-start
  0.0 31.4 %shard_map.82 = f32[24,1,128]{2,1,0:T(1,128)} custom-call(bf16[1,12,128,128]{3,2,1,0:T(8,128)(2,1)} %feat.1, s32[4]{0:T(128)} %offsets.1, bf16[3,3,162,128]{3,2,1,0:T(8,128)(2,1)} %w_one.1, f32[1,128]{1,0:T(1,128)} %bitcast.6, bf16[3,3,128,128]{3,2,1,0:T(8,128)(2,1)} %w_two.1, f32[1,128]{1,0:T(1,128)} %bitcast.7, bf16[3,3,2,128]{3,2,1,0:T(2,128)(2,1)} %bitcast.5), custom_call_target="tpu_custom_call" | custom-call | tf_op jit(solution)/shard_map/pallas_call | solution.py:309
  31.4 0.0 copy-done
  31.4 1.3 %add.3 = f32[2,1,12,128]{3,1,2,0:T(1,128)} add(f32[2,1,12,128]{3,1,2,0:T(1,128)S(1)} %copy-done, f32[2,1,12,128]{3,1,2,0:T(1,128)} %bitcast.4) | non-fusion elementwise | flops 3072 | bytes 36864 | tf_op jit(solution)/shard_map/add | solution.py:335
Async XLA Ops:
  0.0 31.4 %copy-start = (f32[2,1,12,128]{3,1,2,0:T(1,128)S(1)}, f32[2,1,12,128]{3,1,2,0:T(1,128)}, u32[]{:S(2)}) copy-start(f32[2,1,12,128]{3,1,2,0:T(1,128)} %param.10) | copy-start | bytes 36868
where the time goes:
time: 33.2 us; the launch traced here: 32.7 us
  Pallas kernels  31.4 us (95%)
  other arithmetic  1.32 us (4%)
    pallas_call x1, Pallas kernels, body(): pl.pallas_call(functools.partial(kernel, secs, strips), out_shape=jax.Sha...  31.4 us
    add x1, other arithmetic, body(): return state + delta.reshape(state.shape)  1.32 us

commit v1 on v0

v1 whole, which is shorter than its diff:
```python
import functools

import jax
import jax.numpy as jnp
from jax import lax
from jax.experimental import pallas as pl
from jax.experimental.pallas import tpu as pltpu
from jax.sharding import PartitionSpec as P

SIDE = 9
STEP = 3
PAIR = 2
TAPS = 9
SPAN = TAPS + 1
LEFT = SPAN + STEP
EDGE = SIDE + 1
HALO = EDGE // PAIR
HBM = pl.BlockSpec(memory_space=pltpu.HBM)
VMEM = pl.BlockSpec(memory_space=pltpu.VMEM)
MESH = pl.DeviceIdType.MESH


def group_of(rows):
    return max(g for g in range(1, 8) if rows % g == 0)


def when(cond, act):
    if cond is None:
        act()
    else:
        pl.when(cond)(act)


def both(x, y):
    return y if x is None else x & y


def convolve(sources, weight, bias, target):
    rows, cols, width = target.shape
    depth = sources[0].shape[2]
    group = group_of(rows)
    at_col = lax.broadcasted_iota(jnp.int32, (cols, width), 0)

    def step(g, carry):
        base = g * group
        taken = jnp.concatenate(
            [s[pl.ds(base + d, group)].reshape(group * cols, depth) for d in range(3) for s in sources], axis=1
        )
        sums = jnp.dot(taken, weight[...], preferred_element_type=jnp.float32)
        for i in range(group):
            one = sums[i * cols:(i + 1) * cols]
            before = jnp.where(at_col == 0, 0.0, pltpu.roll(one[:, :width], 1, 0))
            after = jnp.where(at_col == cols - 1, 0.0, pltpu.roll(one[:, 2 * width:], cols - 1, 0))
            total = one[:, width:2 * width] + before + after + bias[...]
            target[base + i] = jnp.maximum(total, 0.0).astype(target.dtype)
        return carry

    lax.fori_loop(0, rows // group, step, 0)


def skewed(block, shift):
    rows, cols = block.shape
    pieces = []
    start = 0
    for top in range(0, rows, 8):
        if (shift + top) % cols + 7 > cols:
            if top > start:
                pieces.append(pltpu.roll(block[start:top], (shift + start) % cols, 1, stride=1, stride_axis=0))
            crossing = pltpu.roll(block[top:top + 8], (shift + top - 8) % cols, 1, stride=1, stride_axis=0)
            pieces.append(pltpu.roll(crossing, 8, 1))
            start = top + 8
    if start < rows:
        pieces.append(pltpu.roll(block[start:], (shift + start) % cols, 1, stride=1, stride_axis=0))
    return jnp.concatenate(pieces, axis=0)


def kernel(secs, strips, feat, offsets, w_one, b_one, w_two, b_two, w_three, out,
           mine, near, far, met, corr, hid_one, hid_two, held_one, held_two, held_three, bias_one, bias_two, moved,
           wide_one, wide_two, thirds, direct_recv, relay_recv, beyond_recv, beside_recv, own_recv, send_sem, local_sem):
    rows, cols, chans = feat.shape[1:]
    hid = w_two.shape[3]
    planes = w_one.shape[2] // 2
    count = rows // PAIR
    first = count - HALO
    sec, strip = lax.axis_index("sec"), lax.axis_index("strip")
    odd = lax.rem(sec, 2)
    partner = sec + 1 - 2 * odd
    relay_to, relay_from = sec + 2 - 4 * odd, sec - 2 + 4 * odd
    has_to = (relay_to >= 0) & (relay_to < secs)
    has_from = (relay_from >= 0) & (relay_from < secs)
    has_low, has_high = strip > 0, strip < strips - 1
    core = lax.rem(strip, 2)
    beyond, beside = strip - 1 + 2 * core, strip + 1 - 2 * core
    has_beyond = (beyond >= 0) & (beyond < strips)

    barrier = pltpu.get_barrier_semaphore()
    for cond, a, b in (
        (None, partner, strip), (has_from, relay_from, strip), (None, sec, beside), (has_beyond, sec, beyond),
    ):
        when(cond, lambda a=a, b=b: pl.semaphore_signal(barrier, inc=1, device_id=(a, b), device_id_type=MESH))

    loads = [
        pltpu.make_async_copy(src, dst, local_sem.at[i])
        for i, (src, dst) in enumerate((
            (feat.at[0], mine.at[pl.ds(LEFT + STEP, rows)]), (w_one, held_one), (w_two, held_two), (w_three, held_three),
            (b_one, bias_one), (b_two, bias_two), (offsets, moved),
        ))
    ]
    for load in loads:
        load.start()
    pl.semaphore_wait(barrier, 2 + has_to.astype(jnp.int32) + has_beyond.astype(jnp.int32))

    def remote(src, dst, send, recv, a, b):
        return pltpu.make_async_remote_copy(
            src_ref=src, dst_ref=dst, send_sem=send_sem.at[send], recv_sem=recv, device_id=(a, b), device_id_type=MESH
        )

    def top_of(k):
        return jnp.where(core == 0, PAIR * k, rows - PAIR - PAIR * k)

    def direct(k):
        at = top_of(k)
        return remote(feat.at[0, pl.ds(at, PAIR)], near.at[pl.ds(EDGE + at, PAIR)], 0, direct_recv.at[k], partner, strip)

    def relay(k):
        at = pl.ds(EDGE + top_of(k), PAIR)
        return remote(near.at[at], far.at[at], 1, relay_recv.at[k], relay_to, strip)

    def to_beyond(slot, s, k, length):
        at = top_of(k) + core * (PAIR - length)
        to = EDGE + at + rows - 2 * rows * core
        return remote(
            slot.at[pl.ds(EDGE + at, length)], slot.at[pl.ds(to, length)], 2 + s, beyond_recv.at[s, k], sec, beyond
        )

    def to_beside(slot, s, k, length):
        at = top_of(k) + (1 - core) * (PAIR - length)
        to = EDGE + at - rows + 2 * rows * core
        return remote(
            slot.at[pl.ds(EDGE + at, length)], slot.at[pl.ds(to, length)], 4 + s, beside_recv.at[s, k - first], sec, beside
        )

    def each_start(k, carry):
        direct(k).start()
        return carry

    lax.fori_loop(0, count, each_start, 0)
    own_low = remote(feat.at[0, pl.ds(0, STEP)], mine.at[pl.ds(LEFT + STEP + rows, STEP)], 6, own_recv.at[0], sec, strip - 1)
    own_high = remote(feat.at[0, pl.ds(rows - STEP, STEP)], mine.at[pl.ds(LEFT, STEP)], 7, own_recv.at[1], sec, strip + 1)
    when(has_low, own_low.start)
    when(has_high, own_high.start)

    zero = jnp.zeros((LEFT,) + mine.shape[1:], mine.dtype)
    mine[0:LEFT] = zero
    mine[LEFT + rows + 2 * STEP:] = zero
    for slot in (near, far):
        slot[0] = zero[0]
        slot[slot.shape[0] - 1] = zero[0]

    @pl.when(jnp.logical_not(has_low))
    def _():
        mine[LEFT:LEFT + STEP] = zero[:STEP]

    @pl.when(jnp.logical_not(has_high))
    def _():
        mine[LEFT + STEP + rows:LEFT + 2 * STEP + rows] = zero[:STEP]

    @pl.when(jnp.logical_not(has_beyond))
    def _():
        for s in range(2):
            met[s, pl.ds(core * (EDGE + rows), EDGE)] = jnp.zeros((EDGE, cols, cols), met.dtype)

    scale = chans ** (-0.5)
    lane = lax.broadcasted_iota(jnp.int32, (cols, cols), 1)
    col = lax.broadcasted_iota(jnp.int32, (cols, cols), 0)
    flip = (lane + col == cols - 1).astype(mine.dtype)
    other = cols - 1 - col + lax.rem(lane, TAPS) - 4
    gain = jnp.where((other >= 0) & (other < cols) & (lane < planes), scale, 0.0)

    def turn(r, carry):
        mine[r] = jnp.dot(flip, mine[r], preferred_element_type=jnp.float32).astype(mine.dtype)
        return carry

    for load in loads:
        load.wait()
    lax.fori_loop(LEFT + STEP, LEFT + STEP + rows, turn, 0)
    for d in range(3):
        thirds[8 * d:8 * d + 8] = jnp.zeros((8, hid), thirds.dtype)
        for e in range(3):
            thirds[8 * d + 4 - 2 * e:8 * d + 6 - 2 * e] = held_three[d, e].astype(thirds.dtype)
    for d in range(2 * 3):
        wide_one[d * cols + planes // 16 * 16:(d + 1) * cols] = jnp.zeros((cols - planes // 16 * 16, 3 * hid), wide_one.dtype)
    for d in range(3):
        for e in range(3):
            at = pl.ds((2 - e) * hid, hid)
            for j in range(2):
                wide_one[pl.ds((2 * d + j) * cols, planes), at] = held_one[d, e, j * planes:(j + 1) * planes]
            wide_two[pl.ds(d * hid, hid), at] = held_two[d, e]

    when(has_low, own_high.wait_recv)
    when(has_high, own_low.wait_recv)
    lax.fori_loop(LEFT, LEFT + STEP, turn, 0)
    lax.fori_loop(LEFT + STEP + rows, LEFT + 2 * STEP + rows, turn, 0)

    below = jnp.where(sec > 0, -moved[jnp.maximum(sec - 1, 0)], 0)
    above = jnp.where(sec < secs - 1, moved[sec], 0)
    shifts = (jnp.where(odd == 1, below, above), jnp.where(odd == 1, above, below))
    slots = (near, far)

    def meet(s, w):
        here = mine[pl.ds(w + LEFT - SPAN - 1 - shifts[s], SPAN)].reshape(SPAN * cols, chans)
        there = slots[s][pl.ds(w, PAIR)].reshape(PAIR * cols, chans)
        tile = lax.dot_general(here, there, (((1,), (1,)), ((), ())), preferred_element_type=jnp.float32)
        for u in range(PAIR):
            def block(t):
                j = TAPS - 1 - t + u
                return skewed(tile[j * cols:(j + 1) * cols, u * cols:(u + 1) * cols], t * TAPS + 5)

            found = block(0)
            for t in range(1, TAPS):
                found = jnp.where(lane >= t * TAPS, block(t), found)
            met[s, w + u] = (found * gain).astype(met.dtype)

    def forward(s, k):
        slot = slots[s]
        when(has_beyond & (k < HALO - 1), lambda: to_beyond(slot, s, k, PAIR).start())
        when(has_beyond & (k == HALO - 1), lambda: to_beyond(slot, s, k, PAIR - 1).start())
        when(k > first, lambda: to_beside(slot, s, k, PAIR).start())
        when(k == first, lambda: to_beside(slot, s, k, PAIR - 1).start())

    def from_beyond(s, k):
        when(k < HALO - 1, lambda: to_beyond(slots[s], s, k, PAIR).wait_recv())
        when(k == HALO - 1, lambda: to_beyond(slots[s], s, k, PAIR - 1).wait_recv())
        meet(s, jnp.where(core == 0, EDGE - PAIR - PAIR * k, EDGE + rows + PAIR * k))

    def from_beside(s, k):
        when(k > first, lambda: to_beside(slots[s], s, k, PAIR).wait_recv())
        when(k == first, lambda: to_beside(slots[s], s, k, PAIR - 1).wait_recv())
        meet(s, jnp.where(core == 0, EDGE + 2 * rows - PAIR - PAIR * k, EDGE - rows + PAIR * k))

    def stage(i, carry):
        @pl.when(i < count)
        def _():
            direct(i).wait_recv()
            when(has_to, lambda: relay(i).start())
            forward(0, i)
            meet(0, EDGE + top_of(i))

        when((i - 1 >= first) & (i - 1 < count), lambda: from_beside(0, i - 1))
        when(has_beyond & (i - 2 >= 0) & (i - 2 < HALO), lambda: from_beyond(0, i - 2))

        @pl.when(has_from & (i - 1 >= 0) & (i - 1 < count))
        def _():
            relay(i - 1).wait_recv()
            forward(1, i - 1)
            meet(1, EDGE + top_of(i - 1))

        when(has_from & (i - 3 >= first) & (i - 3 < count), lambda: from_beside(1, i - 3))
        when(has_from & has_beyond & (i - 4 >= 0) & (i - 4 < HALO), lambda: from_beyond(1, i - 4))
        return carry

    lax.fori_loop(0, max(count + 3, HALO + 4), stage, 0)

    def gather(s, at):
        def one(e, carry):
            found = met[s, e + STEP + shifts[s]]
            for a in range(1, TAPS):
                found = jnp.where(lane >= a * TAPS, met[s, e + STEP + shifts[s] + a], found)
            corr[at, e] = found
            return carry

        lax.fori_loop(0, rows + 2 * STEP, one, 0)

    gather(0, 1 - odd)
    when(has_from, lambda: gather(1, odd))

    @pl.when(jnp.logical_not(has_from))
    def _():
        corr[odd] = jnp.zeros(corr.shape[1:], corr.dtype)

    convolve((corr.at[0], corr.at[1]), wide_one, bias_one, hid_one)

    @pl.when(strip == 0)
    def _():
        hid_one[0:2] = jnp.zeros((2, cols, hid), hid_one.dtype)

    @pl.when(strip == strips - 1)
    def _():
        hid_one[rows + 2:] = jnp.zeros((2, cols, hid), hid_one.dtype)

    convolve((hid_one,), wide_two, bias_two, hid_two)

    @pl.when(strip == 0)
    def _():
        hid_two[0:1] = jnp.zeros((1, cols, hid), hid_two.dtype)

    @pl.when(strip == strips - 1)
    def _():
        hid_two[rows + 1:] = jnp.zeros((1, cols, hid), hid_two.dtype)

    taps = lax.dot_general(
        thirds[...].astype(hid_two.dtype), hid_two[...].reshape((rows + 2) * cols, hid), (((1,), (1,)), ((), ())),
        preferred_element_type=jnp.float32,
    )
    at_lane = lax.broadcasted_iota(jnp.int32, (8, cols), 1)
    found = []
    for r in range(rows):
        total = sum(taps[8 * d:8 * d + 8, (r + d) * cols:(r + d + 1) * cols] for d in range(3))
        before = jnp.where(at_lane == 0, 0.0, pltpu.roll(total, 1, 1))
        after = jnp.where(at_lane == cols - 1, 0.0, pltpu.roll(total, cols - 1, 1))
        found.append(before[0:2] + total[2:4] + after[4:6])
    turned = jnp.dot(
        jnp.concatenate(found, axis=0), flip.astype(jnp.float32),
        preferred_element_type=jnp.float32, precision=lax.Precision.HIGHEST,
    )
    for r in range(rows):
        for p in range(2):
            out[p * rows + r] = turned[2 * r + p:2 * r + p + 1]

    def sent(slot, length, send, a, b):
        at = pl.ds(EDGE, length)
        return remote(slot.at[at], slot.at[at], send, direct_recv.at[0], a, b).wait_send

    sent(near, rows, 0, partner, strip)()
    when(has_to, sent(near, rows, 1, relay_to, strip))
    for s, known in ((0, None), (1, has_from)):
        when(both(known, has_beyond), sent(slots[s], SIDE, 2 + s, sec, beyond))
        when(known, sent(slots[s], SIDE, 4 + s, sec, beside))
    when(has_low, own_low.wait_send)
    when(has_high, own_high.wait_send)


def body(secs, strips, features, offsets, state, w_first, b_first, w_second, b_second, w_third):
    _, rows, cols, chans = features.shape
    hid = w_first.shape[3]
    parts = w_third.shape[3]
    bf16 = jnp.bfloat16
    count = rows // PAIR
    thirds = jnp.transpose(w_third, (0, 1, 3, 2))
    dma = pltpu.SemaphoreType.DMA
    delta = pl.pallas_call(
        functools.partial(kernel, secs, strips),
        out_shape=jax.ShapeDtypeStruct((parts * rows, 1, cols), jnp.float32),
        in_specs=[HBM] * 7,
        out_specs=VMEM,
        scratch_shapes=[
            pltpu.VMEM((rows + 2 * STEP + 2 * LEFT, cols, chans), bf16),
            pltpu.VMEM((rows + 2 * EDGE, cols, chans), bf16),
            pltpu.VMEM((rows + 2 * EDGE, cols, chans), bf16),
            pltpu.VMEM((2, rows + 2 * EDGE, cols, cols), bf16),
            pltpu.VMEM((2, rows + 2 * STEP, cols, cols), bf16),
            pltpu.VMEM((rows + 4, cols, hid), bf16),
            pltpu.VMEM((rows + 2, cols, hid), bf16),
            pltpu.VMEM(w_first.shape, bf16),
            pltpu.VMEM(w_second.shape, bf16),
            pltpu.VMEM(thirds.shape, bf16),
            pltpu.VMEM((1, hid), jnp.float32),
            pltpu.VMEM((1, hid), jnp.float32),
            pltpu.SMEM(offsets.shape, jnp.int32),
            pltpu.VMEM((6 * cols, 3 * hid), bf16),
            pltpu.VMEM((3 * hid, 3 * hid), bf16),
            pltpu.VMEM((24, hid), jnp.float32),
            dma((count,)),
            dma((count,)),
            dma((2, HALO)),
            dma((2, HALO)),
            dma((2,)),
            dma((8,)),
            dma((7,)),
        ],
        compiler_params=pltpu.CompilerParams(collective_id=0, has_side_effects=True, vmem_limit_bytes=24 << 20),
    )(features, offsets, w_first, b_first.reshape(1, hid), w_second, b_second.reshape(1, hid), thirds)
    return state + delta.reshape(state.shape)


def solution(mesh):
    secs, strips = mesh.shape["sec"], mesh.shape["strip"]
    in_specs = (
        P("sec", "strip", None, None),
        P(),
        P(None, "sec", "strip", None),
        P(),
        P(),
        P(),
        P(),
        P(),
    )
    out_specs = P(None, "sec", "strip", None)
    return jax.shard_map(functools.partial(body, secs, strips), mesh=mesh, in_specs=in_specs, out_specs=out_specs, check_vma=False)
```

time: 33.2 us -> 38.5 us (1.16)
  local copies, waits for them, and re-layouts: 0.01 us -> 4.3 us
  Pallas kernels: 31.4 us -> 33.3 us
  other arithmetic: 1.32 us -> 0.61 us
    unnamed x2 -> x16, local copies, waits for them, and re-layouts: 0.01 us -> 4.3 us
    pallas_call x1, Pallas kernels: 31.4 us -> 33.3 us  [body(): pl.pallas_call(functools.partial(kernel, secs, strips), out_shape=jax.Sha...]
    add x1, other arithmetic: 1.32 us -> 0.61 us  [body(): return state + delta.reshape(state.shape)]
where the time goes in v1:
time: 38.5 us; the launch traced here: 38.3 us
  Pallas kernels  33.3 us (86%)
  local copies, waits for them, and re-layouts  4.3 us (11%)
  other arithmetic  0.61 us (2%)
    pallas_call x1, Pallas kernels, body(): pl.pallas_call(functools.partial(kernel, secs, strips), out_shape=jax.Sha...  33.3 us
    unnamed x16, local copies, waits for them, and re-layouts  4.3 us

profile of v1, /device:TPU:19, one launch (start us, length us, event | category | flops | bytes accessed | tf_op | source)
XLA Modules:
  0.0 38.3 jit_solution(11340044453286223518)
XLA Ops:
  0.0 0.0 copy-start.3
  0.0 0.0 copy-start.4
  0.0 0.0 copy-start.5
  0.0 0.7 %copy-done.3 = bf16[3,3,128,2]{2,3,1,0:T(2,128)(2,1)S(1)} copy-done((bf16[3,3,128,2]{2,3,1,0:T(2,128)(2,1)S(1)}, bf16[3,3,128,2]{2,3,1,0:T(2,128)(2,1)}, u32[]{:S(2)}) %copy-start.3) | copy-done | bytes 4632
  0.7 0.0 copy-done.4
  0.7 0.0 copy-done.5
  0.7 0.0 copy-start
  0.7 1.0 %copy-done = bf16[1,12,128,128]{3,2,1,0:T(8,128)(2,1)S(1)} copy-done((bf16[1,12,128,128]{3,2,1,0:T(8,128)(2,1)S(1)}, bf16[1,12,128,128]{3,2,1,0:T(8,128)(2,1)}, u32[]{:S(2)}) %copy-start) | copy-done | bytes 393240
  1.7 0.0 copy-start.1
  1.7 1.0 %copy-done.1 = bf16[3,3,162,128]{3,2,1,0:T(8,128)(2,1)S(1)} copy-done((bf16[3,3,162,128]{3,2,1,0:T(8,128)(2,1)S(1)}, bf16[3,3,162,128]{3,2,1,0:T(8,128)(2,1)}, u32[]{:S(2)}) %copy-start.1) | copy-done | bytes 373272
  2.7 0.0 copy-start.2
  2.7 1.0 %copy-done.2 = bf16[3,3,128,128]{3,2,1,0:T(8,128)(2,1)S(1)} copy-done((bf16[3,3,128,128]{3,2,1,0:T(8,128)(2,1)S(1)}, bf16[3,3,128,128]{3,2,1,0:T(8,128)(2,1)}, u32[]{:S(2)}) %copy-start.2) | copy-done | bytes 294936
  3.6 0.0 copy-start.6
  3.6 0.7 %copy-done.6 = f32[128]{0:T(128)S(1)} copy-done((f32[128]{0:T(128)S(1)}, f32[128]{0:T(128)}, u32[]{:S(2)}) %copy-start.6) | copy-done | bytes 536
  4.3 0.0 copy-start.7
  4.3 33.3 %shard_map.82 = f32[24,1,128]{2,1,0:T(1,128)S(1)} custom-call(bf16[1,12,128,128]{3,2,1,0:T(8,128)(2,1)S(1)} %copy-done, s32[4]{0:T(128)S(1)} %copy-done.4, bf16[3,3,162,128]{3,2,1,0:T(8,128)(2,1)S(1)} %copy-done.1, f32[1,128]{1,0:T(1,128)S(1)} %bitcast.6, bf16[3,3,128,128]{3,2,1,0:T(8,128)(2,1)S(1)} %copy-done.2, f32[1,128]{1,0:T(1,128)S(1)} %bitcast.7, ...), custom_call_target="tpu_custom_call" | custom-call | tf_op jit(solution)/shard_map/pallas_call | solution.py:341
  37.6 0.0 copy-done.7
  37.6 0.6 %add.3 = f32[2,1,12,128]{3,1,2,0:T(1,128)} add(f32[2,1,12,128]{3,1,2,0:T(1,128)S(1)} %copy-done.7, f32[2,1,12,128]{3,1,2,0:T(1,128)S(1)} %bitcast.4) | non-fusion elementwise | flops 3072 | bytes 36864 | tf_op jit(solution)/shard_map/add | solution.py:373
Async XLA Ops:
  0.0 0.7 %copy-start.3 = (bf16[3,3,128,2]{2,3,1,0:T(2,128)(2,1)S(1)}, bf16[3,3,128,2]{2,3,1,0:T(2,128)(2,1)}, u32[]{:S(2)}) copy-start(bf16[3,3,128,2]{2,3,1,0:T(2,128)(2,1)} %param.15) | copy-start | bytes 13828
  0.0 0.7 %copy-start.4 = (s32[4]{0:T(128)S(1)}, s32[4]{0:T(128)}, u32[]{:S(2)}) copy-start(s32[4]{0:T(128)} %offsets.1) | copy-start | bytes 52
  0.0 0.7 %copy-start.5 = (f32[128]{0:T(128)S(1)}, f32[128]{0:T(128)}, u32[]{:S(2)}) copy-start(f32[128]{0:T(128)} %param.12) | copy-start | bytes 1540
  0.7 1.0 %copy-start = (bf16[1,12,128,128]{3,2,1,0:T(8,128)(2,1)S(1)}, bf16[1,12,128,128]{3,2,1,0:T(8,128)(2,1)}, u32[]{:S(2)}) copy-start(bf16[1,12,128,128]{3,2,1,0:T(8,128)(2,1)} %feat.1) | copy-start | bytes 1179652
  1.7 1.0 %copy-start.1 = (bf16[3,3,162,128]{3,2,1,0:T(8,128)(2,1)S(1)}, bf16[3,3,162,128]{3,2,1,0:T(8,128)(2,1)}, u32[]{:S(2)}) copy-start(bf16[3,3,162,128]{3,2,1,0:T(8,128)(2,1)} %w_one.1) | copy-start | bytes 1119748
  2.7 1.0 %copy-start.2 = (bf16[3,3,128,128]{3,2,1,0:T(8,128)(2,1)S(1)}, bf16[3,3,128,128]{3,2,1,0:T(8,128)(2,1)}, u32[]{:S(2)}) copy-start(bf16[3,3,128,128]{3,2,1,0:T(8,128)(2,1)} %w_two.1) | copy-start | bytes 884740
  3.6 0.7 %copy-start.6 = (f32[128]{0:T(128)S(1)}, f32[128]{0:T(128)}, u32[]{:S(2)}) copy-start(f32[128]{0:T(128)} %param.14) | copy-start | bytes 1540
  4.3 33.3 %copy-start.7 = (f32[2,1,12,128]{3,1,2,0:T(1,128)S(1)}, f32[2,1,12,128]{3,1,2,0:T(1,128)}, u32[]{:S(2)}) copy-start(f32[2,1,12,128]{3,1,2,0:T(1,128)} %param.10) | copy-start | bytes 36868

commit v2 on v1

v2 whole, which is shorter than its diff:
```python
import functools

import jax
import jax.numpy as jnp
from jax import lax
from jax.experimental import pallas as pl
from jax.experimental.pallas import tpu as pltpu
from jax.sharding import PartitionSpec as P

SIDE = 9
STEP = 3
PAIR = 2
TAPS = 9
SPAN = TAPS + 1
LEFT = SPAN + STEP
EDGE = SIDE + 1
HALO = EDGE // PAIR
WINDOW = 16
SLOTS = 8
QUAD = 2 * PAIR
RELAYED = 2
BITS = 4
HBM = pl.BlockSpec(memory_space=pltpu.HBM)
VMEM = pl.BlockSpec(memory_space=pltpu.VMEM)
MESH = pl.DeviceIdType.MESH


def group_of(rows):
    return max(g for g in range(1, 8) if rows % g == 0)


def when(cond, act):
    if cond is None:
        act()
    else:
        pl.when(cond)(act)


def both(x, y):
    return y if x is None else x & y


def plan(rows):
    count = rows // PAIR
    tasks = {}
    for w in range(0, rows + 2 * EDGE, QUAD):
        ready = []
        for at in (w, w + PAIR):
            if at < EDGE:
                ready.append((EDGE - PAIR - at) // PAIR + 2)
            elif at >= EDGE + rows:
                ready.append((EDGE + 2 * rows - PAIR - at) // PAIR + 1)
            else:
                ready.append((at - EDGE) // PAIR)
        tasks.setdefault(max(ready), []).append(w // QUAD + 1)
    stages = max(max(tasks) + 1, count)
    width = max(len(found) for found in tasks.values())
    return [[(tasks.get(i, []) + [0] * width)[q] for i in range(stages)] for q in range(width)]


def convolve(sources, weight, bias, target):
    rows, cols, width = target.shape
    depth = sources[0].shape[2]
    group = group_of(rows)
    at_col = lax.broadcasted_iota(jnp.int32, (cols, width), 0)

    def step(g, carry):
        base = g * group
        taken = jnp.concatenate(
            [s[pl.ds(base + d, group)].reshape(group * cols, depth) for d in range(3) for s in sources], axis=1
        )
        sums = jnp.dot(taken, weight[...], preferred_element_type=jnp.float32)
        for i in range(group):
            one = sums[i * cols:(i + 1) * cols]
            before = jnp.where(at_col == 0, 0.0, pltpu.roll(one[:, :width], 1, 0))
            after = jnp.where(at_col == cols - 1, 0.0, pltpu.roll(one[:, 2 * width:], cols - 1, 0))
            total = one[:, width:2 * width] + before + after + bias[...]
            target[base + i] = jnp.maximum(total, 0.0).astype(target.dtype)
        return carry

    lax.fori_loop(0, rows // group, step, 0)


def kernel(secs, strips, feat, offsets, w_one, b_one, w_two, b_two, w_three, out,
           mine, wide, met, twin, corr, hid_one, hid_two, held_one, held_two, held_three, bias_one, bias_two, moved,
           wide_one, wide_two, thirds, direct_recv, relay_recv, beyond_recv, beside_recv, own_recv, send_sem, local_sem):
    rows, cols, chans = feat.shape[1:]
    hid = w_two.shape[3]
    planes = w_one.shape[2] // 2
    count = rows // PAIR
    first = count - HALO
    sec, strip = lax.axis_index("sec"), lax.axis_index("strip")
    odd = lax.rem(sec, 2)
    partner = sec + 1 - 2 * odd
    relay_to, relay_from = sec + 2 - 4 * odd, sec - 2 + 4 * odd
    has_to = (relay_to >= 0) & (relay_to < secs)
    has_from = (relay_from >= 0) & (relay_from < secs)
    has_low, has_high = strip > 0, strip < strips - 1
    core = lax.rem(strip, 2)
    beyond, beside = strip - 1 + 2 * core, strip + 1 - 2 * core
    has_beyond = (beyond >= 0) & (beyond < strips)

    barrier = pltpu.get_barrier_semaphore()
    for cond, a, b in (
        (None, partner, strip), (has_from, relay_from, strip), (None, sec, beside), (has_beyond, sec, beyond),
    ):
        when(cond, lambda a=a, b=b: pl.semaphore_signal(barrier, inc=1, device_id=(a, b), device_id_type=MESH))

    loads = [
        pltpu.make_async_copy(src, dst, local_sem.at[i])
        for i, (src, dst) in enumerate((
            (feat.at[0], mine.at[pl.ds(LEFT + STEP, rows)]), (w_one, held_one), (w_two, held_two), (w_three, held_three),
            (b_one, bias_one), (b_two, bias_two), (offsets, moved),
        ))
    ]
    for load in loads:
        load.start()
    pl.semaphore_wait(barrier, 2 + has_to.astype(jnp.int32) + has_beyond.astype(jnp.int32))

    def remote(src, dst, send, recv, a, b):
        return pltpu.make_async_remote_copy(
            src_ref=src, dst_ref=dst, send_sem=send_sem.at[send], recv_sem=recv, device_id=(a, b), device_id_type=MESH
        )

    def top_of(k):
        return jnp.where(core == 0, PAIR * k, rows - PAIR - PAIR * k)

    def direct(k):
        at = top_of(k)
        return remote(feat.at[0, pl.ds(at, PAIR)], wide.at[0, pl.ds(EDGE + at, PAIR)], 0, direct_recv.at[k], partner, strip)

    def relay(k):
        at = pl.ds(EDGE + top_of(k), PAIR)
        return remote(wide.at[0, at], wide.at[1, at], 1, relay_recv.at[k], relay_to, strip)

    def to_beyond(s, k, length):
        at = top_of(k) + core * (PAIR - length)
        to = EDGE + at + rows - 2 * rows * core
        return remote(
            wide.at[s, pl.ds(EDGE + at, length)], wide.at[s, pl.ds(to, length)], 2 + s, beyond_recv.at[s, k], sec, beyond
        )

    def to_beside(s, k, length):
        at = top_of(k) + (1 - core) * (PAIR - length)
        to = EDGE + at - rows + 2 * rows * core
        return remote(
            wide.at[s, pl.ds(EDGE + at, length)], wide.at[s, pl.ds(to, length)], 4 + s, beside_recv.at[s, k - first], sec, beside
        )

    def each_start(k, carry):
        direct(k).start()
        return carry

    lax.fori_loop(0, count, each_start, 0)
    own_low = remote(feat.at[0, pl.ds(0, STEP)], mine.at[pl.ds(LEFT + STEP + rows, STEP)], 6, own_recv.at[0], sec, strip - 1)
    own_high = remote(feat.at[0, pl.ds(rows - STEP, STEP)], mine.at[pl.ds(LEFT, STEP)], 7, own_recv.at[1], sec, strip + 1)
    when(has_low, own_low.start)
    when(has_high, own_high.start)

    zero = jnp.zeros((LEFT,) + mine.shape[1:], mine.dtype)
    mine[0:LEFT] = zero
    mine[LEFT + rows + 2 * STEP:] = zero
    for s in range(2):
        wide[s, 0] = zero[0]
        wide[s, wide.shape[1] - 1] = zero[0]

    @pl.when(jnp.logical_not(has_low))
    def _():
        mine[LEFT:LEFT + STEP] = zero[:STEP]

    @pl.when(jnp.logical_not(has_high))
    def _():
        mine[LEFT + STEP + rows:LEFT + 2 * STEP + rows] = zero[:STEP]

    @pl.when(jnp.logical_not(has_beyond))
    def _():
        for s in range(2):
            wide[s, pl.ds(core * (EDGE + rows), EDGE)] = jnp.zeros((EDGE, cols, chans), wide.dtype)

    scale = chans ** (-0.5)
    lane = lax.broadcasted_iota(jnp.int32, (cols, cols), 1)
    col = lax.broadcasted_iota(jnp.int32, (cols, cols), 0)
    plane = lax.div(lane, TAPS)
    across = lax.rem(lane, TAPS) - 4
    other = col + across
    inside = (other >= 0) & (other < cols) & (lane < planes)
    source = other + WINDOW * plane
    offset = lane - lax.div(col, 8) * 8 + 4

    for load in loads:
        load.wait()
    for d in range(3):
        thirds[8 * d:8 * d + 8] = jnp.zeros((8, hid), thirds.dtype)
        for e in range(3):
            thirds[8 * d + 2 * e:8 * d + 2 * e + 2] = held_three[d, e].astype(thirds.dtype)
    for d in range(2 * 3):
        wide_one[d * cols + planes // 16 * 16:(d + 1) * cols] = jnp.zeros((cols - planes // 16 * 16, 3 * hid), wide_one.dtype)
    for d in range(3):
        for e in range(3):
            at = pl.ds(e * hid, hid)
            for j in range(2):
                wide_one[pl.ds((2 * d + j) * cols, planes), at] = held_one[d, e, j * planes:(j + 1) * planes]
            wide_two[pl.ds(d * hid, hid), at] = held_two[d, e]

    when(has_low, own_high.wait_recv)
    when(has_high, own_low.wait_recv)

    below = jnp.where(sec > 0, -moved[jnp.maximum(sec - 1, 0)], 0)
    above = jnp.where(sec < secs - 1, moved[sec], 0)
    shifts = (jnp.where(odd == 1, below, above), jnp.where(odd == 1, above, below))

    def meet(s, w):
        shift = jnp.where(s == 0, shifts[0], shifts[1])
        for u in range(QUAD):
            row = wide[s, w + u]
            twin[u, 0:cols] = row
            twin[u, cols:] = row
        turned = [
            twin[u, pl.ds(pl.multiple_of(cols - WINDOW * lax.rem(w + u, SLOTS), WINDOW), cols)] for u in range(QUAD)
        ]
        slot = lax.rem(w, 2 * SLOTS)
        side = slot // SLOTS
        place = (offset - WINDOW * slot) & (cols - 1)
        here = mine[pl.ds(w + LEFT - SPAN - 1 - shift, SPAN + PAIR)]
        tiles = []
        for v in range(2):
            own = here[v * PAIR:v * PAIR + SPAN].reshape(SPAN * cols, chans)
            there = jnp.concatenate(turned[v * PAIR:(v + 1) * PAIR], axis=0)
            tiles.append(lax.dot_general(own, there, (((1,), (1,)), ((), ())), preferred_element_type=jnp.float32))
        for j in range(SPAN + PAIR):
            kept = met[s, side, w + j]
            for v in range(2):
                r = j - v * PAIR
                if 0 <= r < SPAN:
                    one = tiles[v][r * cols:(r + 1) * cols]
                    for u in range(PAIR):
                        if 0 <= TAPS - 1 - r + u < TAPS:
                            low = WINDOW * (v * PAIR + u)
                            kept = jnp.where((place >= low) & (place < low + WINDOW), one[:, u * cols:(u + 1) * cols], kept)
            met[s, side, w + j] = kept

    def gather(s, at):
        def one(g, carry):
            for i in range(STEP):
                e = g * STEP + i
                start = e + STEP + shifts[s]
                index = (source + WINDOW * start) & (cols - 1)
                upper = ((plane + start) & (2 * SLOTS - 1)) >= SLOTS
                own = e + SPAN + 1 + shifts[s]
                sides = [
                    jnp.take_along_axis(met[s, h, own], index, axis=1, mode="promise_in_bounds") for h in range(2)
                ]
                corr[at, e] = jnp.where(inside, jnp.where(upper, sides[1], sides[0]) * scale, 0.0).astype(corr.dtype)
            return carry

        lax.fori_loop(0, (rows + 2 * STEP) // STEP, one, 0)

    def halo(s, at):
        k_beyond = (EDGE - PAIR - at) // PAIR
        k_beside = (EDGE + 2 * rows - PAIR - at) // PAIR
        low, high = (at < EDGE) & has_beyond, at >= EDGE + rows
        when(low & (k_beyond < HALO - 1), lambda: to_beyond(s, k_beyond, PAIR).wait_recv())
        when(low & (k_beyond == HALO - 1), lambda: to_beyond(s, k_beyond, PAIR - 1).wait_recv())
        when(high & (k_beside > first), lambda: to_beside(s, k_beside, PAIR).wait_recv())
        when(high & (k_beside == first), lambda: to_beside(s, k_beside, PAIR - 1).wait_recv())

    table = plan(rows)
    stages, width = len(table[0]), len(table)
    codes = [sum(v << (BITS * i) for i, v in enumerate(line)) for line in table]

    def step(n, carry):
        q = lax.rem(n, width)
        m = n // width
        s = lax.rem(m, 2)
        j = m // 2
        k = j - RELAYED * s
        known = (s == 0) | has_from

        @pl.when(known & (q == 0) & (k >= 0) & (k < count))
        def _():
            when(s == 0, lambda: direct(k).wait_recv())
            when(s == 1, lambda: relay(k).wait_recv())
            when((s == 0) & has_to, lambda: relay(k).start())
            when(has_beyond & (k < HALO - 1), lambda: to_beyond(s, k, PAIR).start())
            when(has_beyond & (k == HALO - 1), lambda: to_beyond(s, k, PAIR - 1).start())
            when(k > first, lambda: to_beside(s, k, PAIR).start())
            when(k == first, lambda: to_beside(s, k, PAIR - 1).start())

        code = codes[0]
        for i in range(1, width):
            code = jnp.where(q == i, codes[i], code)
        task = lax.shift_right_logical(jnp.int32(code), BITS * jnp.clip(k, 0, stages - 1)) & (2 ** BITS - 1)

        @pl.when(known & (k >= 0) & (k < stages) & (task > 0))
        def _():
            w = QUAD * (task - 1)
            halo(s, w)
            halo(s, w + PAIR)
            meet(s, jnp.where(core == 0, w, rows + 2 * EDGE - QUAD - w))

        when((s == 0) & (q == 0) & (j == stages), lambda: gather(0, 1 - odd))
        return carry

    lax.fori_loop(0, (stages + RELAYED) * 2 * width, step, 0)

    when(has_from, lambda: gather(1, odd))

    @pl.when(jnp.logical_not(has_from))
    def _():
        corr[odd] = jnp.zeros(corr.shape[1:], corr.dtype)

    convolve((corr.at[0], corr.at[1]), wide_one, bias_one, hid_one)

    @pl.when(strip == 0)
    def _():
        hid_one[0:2] = jnp.zeros((2, cols, hid), hid_one.dtype)

    @pl.when(strip == strips - 1)
    def _():
        hid_one[rows + 2:] = jnp.zeros((2, cols, hid), hid_one.dtype)

    convolve((hid_one,), wide_two, bias_two, hid_two)

    @pl.when(strip == 0)
    def _():
        hid_two[0:1] = jnp.zeros((1, cols, hid), hid_two.dtype)

    @pl.when(strip == strips - 1)
    def _():
        hid_two[rows + 1:] = jnp.zeros((1, cols, hid), hid_two.dtype)

    taps = lax.dot_general(
        thirds[...].astype(hid_two.dtype), hid_two[...].reshape((rows + 2) * cols, hid), (((1,), (1,)), ((), ())),
        preferred_element_type=jnp.float32,
    )
    at_lane = lax.broadcasted_iota(jnp.int32, (8, cols), 1)
    found = []
    for r in range(rows):
        total = sum(taps[8 * d:8 * d + 8, (r + d) * cols:(r + d + 1) * cols] for d in range(3))
        before = jnp.where(at_lane == 0, 0.0, pltpu.roll(total, 1, 1))
        after = jnp.where(at_lane == cols - 1, 0.0, pltpu.roll(total, cols - 1, 1))
        found.append(before[0:2] + total[2:4] + after[4:6])
    turned = jnp.concatenate(found, axis=0)
    for r in range(rows):
        for p in range(2):
            out[p * rows + r] = turned[2 * r + p:2 * r + p + 1]

    def sent(s, length, send, a, b):
        at = pl.ds(EDGE, length)
        return remote(wide.at[s, at], wide.at[s, at], send, direct_recv.at[0], a, b).wait_send

    sent(0, rows, 0, partner, strip)()
    when(has_to, sent(0, rows, 1, relay_to, strip))
    for s, known in ((0, None), (1, has_from)):
        when(both(known, has_beyond), sent(s, SIDE, 2 + s, sec, beyond))
        when(known, sent(s, SIDE, 4 + s, sec, beside))
    when(has_low, own_low.wait_send)
    when(has_high, own_high.wait_send)


def body(secs, strips, features, offsets, state, w_first, b_first, w_second, b_second, w_third):
    _, rows, cols, chans = features.shape
    hid = w_first.shape[3]
    parts = w_third.shape[3]
    bf16 = jnp.bfloat16
    count = rows // PAIR
    thirds = jnp.transpose(w_third, (0, 1, 3, 2))
    dma = pltpu.SemaphoreType.DMA
    delta = pl.pallas_call(
        functools.partial(kernel, secs, strips),
        out_shape=jax.ShapeDtypeStruct((parts * rows, 1, cols), jnp.float32),
        in_specs=[HBM] * 7,
        out_specs=VMEM,
        scratch_shapes=[
            pltpu.VMEM((rows + 2 * STEP + 2 * LEFT, cols, chans), bf16),
            pltpu.VMEM((2, rows + 2 * EDGE, cols, chans), bf16),
            pltpu.VMEM((2, 2, rows + 2 * EDGE + SPAN, cols, cols), jnp.float32),
            pltpu.VMEM((QUAD, 2 * cols, chans), bf16),
            pltpu.VMEM((2, rows + 2 * STEP, cols, cols), bf16),
            pltpu.VMEM((rows + 4, cols, hid), bf16),
            pltpu.VMEM((rows + 2, cols, hid), bf16),
            pltpu.VMEM(w_first.shape, bf16),
            pltpu.VMEM(w_second.shape, bf16),
            pltpu.VMEM(thirds.shape, bf16),
            pltpu.VMEM((1, hid), jnp.float32),
            pltpu.VMEM((1, hid), jnp.float32),
            pltpu.SMEM(offsets.shape, jnp.int32),
            pltpu.VMEM((6 * cols, 3 * hid), bf16),
            pltpu.VMEM((3 * hid, 3 * hid), bf16),
            pltpu.VMEM((24, hid), jnp.float32),
            dma((count,)),
            dma((count,)),
            dma((2, HALO)),
            dma((2, HALO)),
            dma((2,)),
            dma((8,)),
            dma((7,)),
        ],
        compiler_params=pltpu.CompilerParams(collective_id=0, has_side_effects=True, vmem_limit_bytes=56 << 20),
    )(features, offsets, w_first, b_first.reshape(1, hid), w_second, b_second.reshape(1, hid), thirds)
    return state + delta.reshape(state.shape)


def solution(mesh):
    secs, strips = mesh.shape["sec"], mesh.shape["strip"]
    in_specs = (
        P("sec", "strip", None, None),
        P(),
        P(None, "sec", "strip", None),
        P(),
        P(),
        P(),
        P(),
        P(),
    )
    out_specs = P(None, "sec", "strip", None)
    return jax.shard_map(functools.partial(body, secs, strips), mesh=mesh, in_specs=in_specs, out_specs=out_specs, check_vma=False)
```

time: 38.5 us -> 31.7 us (0.82)
  local copies, waits for them, and re-layouts: 4.3 us -> 0.01 us
  Pallas kernels: 33.3 us -> 30.1 us
  other arithmetic: 0.61 us -> 1.32 us
    unnamed x16 -> x2, local copies, waits for them, and re-layouts: 4.3 us -> 0.01 us
    pallas_call x1, Pallas kernels: 33.3 us -> 30.1 us  [body(): pl.pallas_call(functools.partial(kernel, secs, strips), out_shape=jax.Sha...]
    add x1, other arithmetic: 0.61 us -> 1.32 us  [body(): return state + delta.reshape(state.shape)]
where the time goes in v2:
time: 31.7 us; the launch traced here: 31.4 us
  Pallas kernels  30.1 us (95%)
  other arithmetic  1.32 us (4%)
    pallas_call x1, Pallas kernels, body(): pl.pallas_call(functools.partial(kernel, secs, strips), out_shape=jax.Sha...  30.1 us
    add x1, other arithmetic, body(): return state + delta.reshape(state.shape)  1.32 us

profile of v2, /device:TPU:19, one launch (start us, length us, event | category | flops | bytes accessed | tf_op | source)
XLA Modules:
  0.0 31.4 jit_solution(1651498005911839727)
XLA Ops:
  0.0 0.0 copy-start
  0.0 30.1 %shard_map.82 = f32[24,1,128]{2,1,0:T(1,128)} custom-call(bf16[1,12,128,128]{3,2,1,0:T(8,128)(2,1)} %feat.1, s32[4]{0:T(128)} %offsets.1, bf16[3,3,162,128]{3,2,1,0:T(8,128)(2,1)} %w_one.1, f32[1,128]{1,0:T(1,128)} %bitcast.6, bf16[3,3,128,128]{3,2,1,0:T(8,128)(2,1)} %w_two.1, f32[1,128]{1,0:T(1,128)} %bitcast.7, bf16[3,3,2,128]{3,2,1,0:T(2,128)(2,1)} %bitcast.5), custom_call_target="tpu_custom_call" | custom-call | tf_op jit(solution)/shard_map/pallas_call | solution.py:369
  30.1 0.0 copy-done
  30.1 1.3 %add.3 = f32[2,1,12,128]{3,1,2,0:T(1,128)} add(f32[2,1,12,128]{3,1,2,0:T(1,128)S(1)} %copy-done, f32[2,1,12,128]{3,1,2,0:T(1,128)} %bitcast.4) | non-fusion elementwise | flops 3072 | bytes 36864 | tf_op jit(solution)/shard_map/add | solution.py:401
Async XLA Ops:
  0.0 30.1 %copy-start = (f32[2,1,12,128]{3,1,2,0:T(1,128)S(1)}, f32[2,1,12,128]{3,1,2,0:T(1,128)}, u32[]{:S(2)}) copy-start(f32[2,1,12,128]{3,1,2,0:T(1,128)} %param.10) | copy-start | bytes 36868

commit v3 on v2

--- a/solution.py
+++ b/solution.py
@@ -15,8 +15,6 @@
 LEFT = SPAN + STEP
 EDGE = SIDE + 1
 HALO = EDGE // PAIR
-WINDOW = 16
-SLOTS = 8
 QUAD = 2 * PAIR
 RELAYED = 2
 BITS = 4
@@ -26,7 +24,7 @@
 
 
 def group_of(rows):
-    return max(g for g in range(1, 8) if rows % g == 0)
+    return max(g for g in range(1, 9) if rows % g == 0)
 
 
 def when(cond, act):
@@ -82,7 +80,7 @@
 
 
 def kernel(secs, strips, feat, offsets, w_one, b_one, w_two, b_two, w_three, out,
-           mine, wide, met, twin, corr, hid_one, hid_two, held_one, held_two, held_three, bias_one, bias_two, moved,
+           mine, wide, met, corr, hid_one, hid_two, held_one, held_two, held_three, bias_one, bias_two, moved,
            wide_one, wide_two, thirds, direct_recv, relay_recv, beyond_recv, beside_recv, own_recv, send_sem, local_sem):
     rows, cols, chans = feat.shape[1:]
     hid = w_two.shape[3]
@@ -180,12 +178,10 @@
     scale = chans ** (-0.5)
     lane = lax.broadcasted_iota(jnp.int32, (cols, cols), 1)
     col = lax.broadcasted_iota(jnp.int32, (cols, cols), 0)
-    plane = lax.div(lane, TAPS)
-    across = lax.rem(lane, TAPS) - 4
-    other = col + across
+    other = col + lax.rem(lane, TAPS) - 4
     inside = (other >= 0) & (other < cols) & (lane < planes)
-    source = other + WINDOW * plane
-    offset = lane - lax.div(col, 8) * 8 + 4
+    source = lane + col - 4
+    offset = lane - col + 4
 
     for load in loads:
         load.wait()
@@ -211,16 +207,8 @@
 
     def meet(s, w):
         shift = jnp.where(s == 0, shifts[0], shifts[1])
-        for u in range(QUAD):
-            row = wide[s, w + u]
-            twin[u, 0:cols] = row
-            twin[u, cols:] = row
-        turned = [
-            twin[u, pl.ds(pl.multiple_of(cols - WINDOW * lax.rem(w + u, SLOTS), WINDOW), cols)] for u in range(QUAD)
-        ]
-        slot = lax.rem(w, 2 * SLOTS)
-        side = slot // SLOTS
-        place = (offset - WINDOW * slot) & (cols - 1)
+        turned = [pltpu.roll(wide[s, w + u], lax.rem(TAPS * (w + u), cols), 0) for u in range(QUAD)]
+        place = (offset - TAPS * w) & (cols - 1)
         here = mine[pl.ds(w + LEFT - SPAN - 1 - shift, SPAN + PAIR)]
         tiles = []
         for v in range(2):
@@ -228,29 +216,27 @@
             there = jnp.concatenate(turned[v * PAIR:(v + 1) * PAIR], axis=0)
             tiles.append(lax.dot_general(own, there, (((1,), (1,)), ((), ())), preferred_element_type=jnp.float32))
         for j in range(SPAN + PAIR):
-            kept = met[s, side, w + j]
-            for v in range(2):
-                r = j - v * PAIR
-                if 0 <= r < SPAN:
-                    one = tiles[v][r * cols:(r + 1) * cols]
-                    for u in range(PAIR):
-                        if 0 <= TAPS - 1 - r + u < TAPS:
-                            low = WINDOW * (v * PAIR + u)
-                            kept = jnp.where((place >= low) & (place < low + WINDOW), one[:, u * cols:(u + 1) * cols], kept)
-            met[s, side, w + j] = kept
+            us = [u for u in range(QUAD) if 0 <= TAPS - 1 - j + u < TAPS]
+            kept = met[s, w + j]
+            found = kept
+            for u in reversed(us):
+                r = j - u // PAIR * PAIR
+                one = tiles[u // PAIR][r * cols:(r + 1) * cols, u % PAIR * cols:(u % PAIR + 1) * cols]
+                found = jnp.where(place < TAPS * (u + 1), one, found)
+            if us[0] > 0:
+                found = jnp.where(place < TAPS * us[0], kept, found)
+            met[s, w + j] = found
 
     def gather(s, at):
         def one(g, carry):
             for i in range(STEP):
                 e = g * STEP + i
                 start = e + STEP + shifts[s]
-                index = (source + WINDOW * start) & (cols - 1)
-                upper = ((plane + start) & (2 * SLOTS - 1)) >= SLOTS
-                own = e + SPAN + 1 + shifts[s]
-                sides = [
-                    jnp.take_along_axis(met[s, h, own], index, axis=1, mode="promise_in_bounds") for h in range(2)
-                ]
-                corr[at, e] = jnp.where(inside, jnp.where(upper, sides[1], sides[0]) * scale, 0.0).astype(corr.dtype)
+                index = (source + TAPS * start) & (cols - 1)
+                moved_row = jnp.take_along_axis(
+                    met[s, e + SPAN + 1 + shifts[s]], index, axis=1, mode="promise_in_bounds"
+                )
+                corr[at, e] = jnp.where(inside, moved_row * scale, 0.0).astype(corr.dtype)
             return carry
 
         lax.fori_loop(0, (rows + 2 * STEP) // STEP, one, 0)
@@ -374,8 +360,7 @@
         scratch_shapes=[
             pltpu.VMEM((rows + 2 * STEP + 2 * LEFT, cols, chans), bf16),
             pltpu.VMEM((2, rows + 2 * EDGE, cols, chans), bf16),
-            pltpu.VMEM((2, 2, rows + 2 * EDGE + SPAN, cols, cols), jnp.float32),
-            pltpu.VMEM((QUAD, 2 * cols, chans), bf16),
+            pltpu.VMEM((2, rows + 2 * EDGE + SPAN, cols, cols), jnp.float32),
             pltpu.VMEM((2, rows + 2 * STEP, cols, cols), bf16),
             pltpu.VMEM((rows + 4, cols, hid), bf16),
             pltpu.VMEM((rows + 2, cols, hid), bf16),
@@ -396,8 +381,8 @@
             dma((8,)),
             dma((7,)),
         ],
-        compiler_params=pltpu.CompilerParams(collective_id=0, has_side_effects=True, vmem_limit_bytes=56 << 20),
-    )(features, offsets, w_first, b_first.reshape(1, hid), w_second, b_second.reshape(1, hid), thirds)
+        compiler_params=pltpu.CompilerParams(collective_id=0, has_side_effects=True, vmem_limit_bytes=24 << 20),
+    )(*(pltpu.with_memory_space_constraint(x, pltpu.HBM) for x in (features, offsets, w_first, b_first.reshape(1, hid), w_second, b_second.reshape(1, hid), thirds)))
     return state + delta.reshape(state.shape)
 
 

time: 31.7 us -> 28.3 us (0.89)
  Pallas kernels: 30.1 us -> 27.5 us
  other arithmetic: 1.32 us -> 0.61 us
    pallas_call x1, Pallas kernels: 30.1 us -> 27.5 us  [body(): pl.pallas_call(functools.partial(kernel, secs, strips), out_shape=jax.Sha...]
    add x1, other arithmetic: 1.32 us -> 0.61 us  [body(): return state + delta.reshape(state.shape)]
where the time goes in v3:
time: 28.3 us; the launch traced here: 28.2 us
  Pallas kernels  27.5 us (97%)
  other arithmetic  0.61 us (2%)
    pallas_call x1, Pallas kernels, body(): pl.pallas_call(functools.partial(kernel, secs, strips), out_shape=jax.Sha...  27.5 us
    add x1, other arithmetic, body(): return state + delta.reshape(state.shape)  0.61 us

profile of v3, /device:TPU:19, one launch (start us, length us, event | category | flops | bytes accessed | tf_op | source)
XLA Modules:
  0.0 28.2 jit_solution(7476786340168335457)
XLA Ops:
  0.0 0.0 copy-start
  0.0 27.5 %shard_map.82 = f32[24,1,128]{2,1,0:T(1,128)S(1)} custom-call(bf16[1,12,128,128]{3,2,1,0:T(8,128)(2,1)} %feat.1, s32[4]{0:T(128)} %offsets.1, bf16[3,3,162,128]{3,2,1,0:T(8,128)(2,1)} %w_one.1, f32[1,128]{1,0:T(1,128)} %bitcast.6, bf16[3,3,128,128]{3,2,1,0:T(8,128)(2,1)} %w_two.1, f32[1,128]{1,0:T(1,128)} %bitcast.7, bf16[3,3,2,128]{3,2,1,0:T(2,128)(2,1)} %bitcast.5), custom_call_target="tpu_custom_call" | custom-call | tf_op jit(solution)/shard_map/pallas_call | solution.py:355
  27.6 0.0 copy-done
  27.6 0.6 %add.3 = f32[2,1,12,128]{3,1,2,0:T(1,128)} add(f32[2,1,12,128]{3,1,2,0:T(1,128)S(1)} %copy-done, f32[2,1,12,128]{3,1,2,0:T(1,128)S(1)} %bitcast.4) | non-fusion elementwise | flops 3072 | bytes 36864 | tf_op jit(solution)/shard_map/add | solution.py:386
Async XLA Ops:
  0.0 27.6 %copy-start = (f32[2,1,12,128]{3,1,2,0:T(1,128)S(1)}, f32[2,1,12,128]{3,1,2,0:T(1,128)}, u32[]{:S(2)}) copy-start(f32[2,1,12,128]{3,1,2,0:T(1,128)} %param.10) | copy-start | bytes 36868

commit v4 on v3

--- a/solution.py
+++ b/solution.py
@@ -17,6 +17,8 @@
 HALO = EDGE // PAIR
 QUAD = 2 * PAIR
 RELAYED = 2
+LATER = 1
+SHORT = 7
 BITS = 4
 HBM = pl.BlockSpec(memory_space=pltpu.HBM)
 VMEM = pl.BlockSpec(memory_space=pltpu.VMEM)
@@ -24,7 +26,7 @@
 
 
 def group_of(rows):
-    return max(g for g in range(1, 9) if rows % g == 0)
+    return max(g for g in range(2, 15, 2) if rows % g == 0)
 
 
 def when(cond, act):
@@ -56,32 +58,29 @@
     return [[(tasks.get(i, []) + [0] * width)[q] for i in range(stages)] for q in range(width)]
 
 
-def convolve(sources, weight, bias, target):
-    rows, cols, width = target.shape
-    depth = sources[0].shape[2]
-    group = group_of(rows)
+def convolve(sources, weight, tail, bias, target, base, group):
+    cols, width = target.shape[1:]
     at_col = lax.broadcasted_iota(jnp.int32, (cols, width), 0)
 
-    def step(g, carry):
-        base = g * group
-        taken = jnp.concatenate(
-            [s[pl.ds(base + d, group)].reshape(group * cols, depth) for d in range(3) for s in sources], axis=1
+    def taken(rows, depths):
+        return jnp.concatenate(
+            [jnp.concatenate([s[base + r + d] for r in rows], axis=0) for d in depths for s in sources], axis=1
         )
-        sums = jnp.dot(taken, weight[...], preferred_element_type=jnp.float32)
-        for i in range(group):
-            one = sums[i * cols:(i + 1) * cols]
-            before = jnp.where(at_col == 0, 0.0, pltpu.roll(one[:, :width], 1, 0))
-            after = jnp.where(at_col == cols - 1, 0.0, pltpu.roll(one[:, 2 * width:], cols - 1, 0))
-            total = one[:, width:2 * width] + before + after + bias[...]
-            target[base + i] = jnp.maximum(total, 0.0).astype(target.dtype)
-        return carry
-
-    lax.fori_loop(0, rows // group, step, 0)
+
+    main = jnp.dot(taken(range(group), range(3)), weight[...], preferred_element_type=jnp.float32)
+    rest = jnp.dot(taken(range(0, group, 2), range(4)), tail[...], preferred_element_type=jnp.float32)
+    for i in range(group):
+        one = main[i * cols:(i + 1) * cols]
+        other = rest[i // 2 * cols:(i // 2 + 1) * cols, i % 2 * width:(i % 2 + 1) * width]
+        before = jnp.where(at_col == 0, 0.0, pltpu.roll(one[:, :width], 1, 0))
+        after = jnp.where(at_col == cols - 1, 0.0, pltpu.roll(other, cols - 1, 0))
+        total = one[:, width:2 * width] + before + after + bias[...]
+        target[base + i] = jnp.maximum(total, 0.0).astype(target.dtype)
 
 
 def kernel(secs, strips, feat, offsets, w_one, b_one, w_two, b_two, w_three, out,
            mine, wide, met, corr, hid_one, hid_two, held_one, held_two, held_three, bias_one, bias_two, moved,
-           wide_one, wide_two, thirds, direct_recv, relay_recv, beyond_recv, beside_recv, own_recv, send_sem, local_sem):
+           main_one, rest_one, main_two, rest_two, thirds, direct_recv, relay_recv, beyond_recv, beside_recv, own_recv, send_sem, local_sem):
     rows, cols, chans = feat.shape[1:]
     hid = w_two.shape[3]
     planes = w_one.shape[2] // 2
@@ -189,14 +188,22 @@
         thirds[8 * d:8 * d + 8] = jnp.zeros((8, hid), thirds.dtype)
         for e in range(3):
             thirds[8 * d + 2 * e:8 * d + 2 * e + 2] = held_three[d, e].astype(thirds.dtype)
-    for d in range(2 * 3):
-        wide_one[d * cols + planes // 16 * 16:(d + 1) * cols] = jnp.zeros((cols - planes // 16 * 16, 3 * hid), wide_one.dtype)
+    for ref in (main_one, rest_one, rest_two):
+        ref[...] = jnp.zeros(ref.shape, ref.dtype)
     for d in range(3):
-        for e in range(3):
-            at = pl.ds(e * hid, hid)
-            for j in range(2):
-                wide_one[pl.ds((2 * d + j) * cols, planes), at] = held_one[d, e, j * planes:(j + 1) * planes]
-            wide_two[pl.ds(d * hid, hid), at] = held_two[d, e]
+        for j, place in ((0, 1 - odd), (1, odd)):
+            part = pl.ds(j * planes, planes)
+            at = pl.ds(pl.multiple_of((2 * d + place) * cols, cols), planes)
+            next_at = pl.ds(pl.multiple_of((2 * d + 2 + place) * cols, cols), planes)
+            for e in range(2):
+                main_one[at, e * hid:(e + 1) * hid] = held_one[d, e, part]
+            rest_one[at, 0:hid] = held_one[d, 2, part]
+            rest_one[next_at, hid:2 * hid] = held_one[d, 2, part]
+        at, next_at = pl.ds(d * hid, hid), pl.ds((d + 1) * hid, hid)
+        for e in range(2):
+            main_two[at, e * hid:(e + 1) * hid] = held_two[d, e]
+        rest_two[at, 0:hid] = held_two[d, 2]
+        rest_two[next_at, hid:2 * hid] = held_two[d, 2]
 
     when(has_low, own_high.wait_recv)
     when(has_high, own_low.wait_recv)
@@ -205,16 +212,23 @@
     above = jnp.where(sec < secs - 1, moved[sec], 0)
     shifts = (jnp.where(odd == 1, below, above), jnp.where(odd == 1, above, below))
 
+    def turned(s, w):
+        return [pltpu.roll(wide[s, w + u], (TAPS * (w + u)) & (cols - 1), 0) for u in range(QUAD)]
+
+    def product(own, there):
+        return lax.dot_general(
+            own.reshape(-1, chans), jnp.concatenate(there, axis=0), (((1,), (1,)), ((), ())),
+            preferred_element_type=jnp.float32,
+        )
+
+    def shift_of(s):
+        return jnp.where(s == 0, shifts[0], shifts[1])
+
     def meet(s, w):
-        shift = jnp.where(s == 0, shifts[0], shifts[1])
-        turned = [pltpu.roll(wide[s, w + u], lax.rem(TAPS * (w + u), cols), 0) for u in range(QUAD)]
+        there = turned(s, w)
         place = (offset - TAPS * w) & (cols - 1)
-        here = mine[pl.ds(w + LEFT - SPAN - 1 - shift, SPAN + PAIR)]
-        tiles = []
-        for v in range(2):
-            own = here[v * PAIR:v * PAIR + SPAN].reshape(SPAN * cols, chans)
-            there = jnp.concatenate(turned[v * PAIR:(v + 1) * PAIR], axis=0)
-            tiles.append(lax.dot_general(own, there, (((1,), (1,)), ((), ())), preferred_element_type=jnp.float32))
+        here = mine[pl.ds(w + LEFT - SPAN - 1 - shift_of(s), SPAN + PAIR)]
+        tiles = [product(here[v * PAIR:v * PAIR + SPAN], there[v * PAIR:(v + 1) * PAIR]) for v in range(2)]
         for j in range(SPAN + PAIR):
             us = [u for u in range(QUAD) if 0 <= TAPS - 1 - j + u < TAPS]
             kept = met[s, w + j]
@@ -227,19 +241,35 @@
                 found = jnp.where(place < TAPS * us[0], kept, found)
             met[s, w + j] = found
 
-    def gather(s, at):
-        def one(g, carry):
-            for i in range(STEP):
-                e = g * STEP + i
-                start = e + STEP + shifts[s]
-                index = (source + TAPS * start) & (cols - 1)
-                moved_row = jnp.take_along_axis(
-                    met[s, e + SPAN + 1 + shifts[s]], index, axis=1, mode="promise_in_bounds"
-                )
-                corr[at, e] = jnp.where(inside, moved_row * scale, 0.0).astype(corr.dtype)
+    def meet_edge(s, w):
+        there = turned(s, w)
+        place = (offset - TAPS * w) & (cols - 1)
+        begin = jnp.where(w <= QUAD, SPAN + PAIR - SHORT, 0)
+        here = mine[pl.ds(w + begin + LEFT - SPAN - 1 - shift_of(s), SHORT)]
+        tiles = [product(here, there[v * PAIR:(v + 1) * PAIR]) for v in range(2)]
+        for r in range(SHORT):
+            j = begin + r
+            low, high = TAPS * jnp.maximum(j - TAPS + 1, 0), TAPS * jnp.minimum(j + 1, QUAD)
+            kept = met[s, w + j]
+            found = tiles[1][r * cols:(r + 1) * cols, cols:]
+            for u in reversed(range(QUAD - 1)):
+                one = tiles[u // PAIR][r * cols:(r + 1) * cols, u % PAIR * cols:(u % PAIR + 1) * cols]
+                found = jnp.where(place < TAPS * (u + 1), one, found)
+            met[s, w + j] = jnp.where((place >= low) & (place < high), found, kept)
+
+    def gather(s, e):
+        index = (source + TAPS * (e + STEP + shifts[s])) & (cols - 1)
+        moved_row = jnp.take_along_axis(met[s, e + SPAN + 1 + shifts[s]], index, axis=1, mode="promise_in_bounds")
+        keep = inside if s == 0 else inside & has_from
+        corr[s, e] = jnp.where(keep, moved_row * scale, 0.0).astype(corr.dtype)
+
+    def gather_some(s, start, end):
+        def some(g, carry):
+            for i in range(PAIR):
+                gather(s, start + g * PAIR + i)
             return carry
 
-        lax.fori_loop(0, (rows + 2 * STEP) // STEP, one, 0)
+        lax.fori_loop(0, (end - start) // PAIR, some, 0)
 
     def halo(s, at):
         k_beyond = (EDGE - PAIR - at) // PAIR
@@ -255,14 +285,11 @@
     codes = [sum(v << (BITS * i) for i, v in enumerate(line)) for line in table]
 
     def step(n, carry):
-        q = lax.rem(n, width)
-        m = n // width
-        s = lax.rem(m, 2)
-        j = m // 2
+        s, j = lax.rem(n, 2), n // 2
         k = j - RELAYED * s
         known = (s == 0) | has_from
 
-        @pl.when(known & (q == 0) & (k >= 0) & (k < count))
+        @pl.when(known & (k >= 0) & (k < count))
         def _():
             when(s == 0, lambda: direct(k).wait_recv())
             when(s == 1, lambda: relay(k).wait_recv())
@@ -272,30 +299,38 @@
             when(k > first, lambda: to_beside(s, k, PAIR).start())
             when(k == first, lambda: to_beside(s, k, PAIR - 1).start())
 
-        code = codes[0]
-        for i in range(1, width):
-            code = jnp.where(q == i, codes[i], code)
-        task = lax.shift_right_logical(jnp.int32(code), BITS * jnp.clip(k, 0, stages - 1)) & (2 ** BITS - 1)
-
-        @pl.when(known & (k >= 0) & (k < stages) & (task > 0))
+        t = k - LATER * s
+
+        @pl.when(known & (t >= 0) & (t < stages))
         def _():
-            w = QUAD * (task - 1)
-            halo(s, w)
-            halo(s, w + PAIR)
-            meet(s, jnp.where(core == 0, w, rows + 2 * EDGE - QUAD - w))
-
-        when((s == 0) & (q == 0) & (j == stages), lambda: gather(0, 1 - odd))
+            tasks = [lax.shift_right_logical(jnp.int32(code), BITS * t) & (2 ** BITS - 1) for code in codes]
+
+            def work(q, carry):
+                task = tasks[0]
+                for i in range(1, width):
+                    task = jnp.where(q == i, tasks[i], task)
+                w = QUAD * (task - 1)
+                halo(s, w)
+                halo(s, w + PAIR)
+                edge = (w <= QUAD) | (w >= rows + EDGE + PAIR)
+                at = jnp.where(core == 0, w, rows + 2 * EDGE - QUAD - w)
+                when(edge, lambda: meet_edge(s, at))
+                when(jnp.logical_not(edge), lambda: meet(s, at))
+                return carry
+
+            lax.fori_loop(0, sum((task > 0).astype(jnp.int32) for task in tasks), work, 0)
+
+        when((s == 0) & (j == stages + 1), lambda: gather_some(0, 0, rows + 2 * STEP))
         return carry
 
-    lax.fori_loop(0, (stages + RELAYED) * 2 * width, step, 0)
-
-    when(has_from, lambda: gather(1, odd))
-
-    @pl.when(jnp.logical_not(has_from))
-    def _():
-        corr[odd] = jnp.zeros(corr.shape[1:], corr.dtype)
-
-    convolve((corr.at[0], corr.at[1]), wide_one, bias_one, hid_one)
+    lax.fori_loop(0, (stages + RELAYED + LATER) * 2, step, 0)
+
+    group = group_of(rows + 4)
+    gather_some(1, 0, group + PAIR)
+    for base in range(0, rows + 4, group):
+        for e in range(base + group + PAIR, min(base + 2 * group + PAIR, rows + 2 * STEP)):
+            gather(1, e)
+        convolve((corr.at[0], corr.at[1]), main_one, rest_one, bias_one, hid_one, base, group)
 
     @pl.when(strip == 0)
     def _():
@@ -305,7 +340,9 @@
     def _():
         hid_one[rows + 2:] = jnp.zeros((2, cols, hid), hid_one.dtype)
 
-    convolve((hid_one,), wide_two, bias_two, hid_two)
+    group = group_of(rows + 2)
+    for base in range(0, rows + 2, group):
+        convolve((hid_one,), main_two, rest_two, bias_two, hid_two, base, group)
 
     @pl.when(strip == 0)
     def _():
@@ -370,8 +407,10 @@
             pltpu.VMEM((1, hid), jnp.float32),
             pltpu.VMEM((1, hid), jnp.float32),
             pltpu.SMEM(offsets.shape, jnp.int32),
-            pltpu.VMEM((6 * cols, 3 * hid), bf16),
-            pltpu.VMEM((3 * hid, 3 * hid), bf16),
+            pltpu.VMEM((6 * cols, 2 * hid), bf16),
+            pltpu.VMEM((8 * cols, 2 * hid), bf16),
+            pltpu.VMEM((3 * hid, 2 * hid), bf16),
+            pltpu.VMEM((4 * hid, 2 * hid), bf16),
             pltpu.VMEM((24, hid), jnp.float32),
             dma((count,)),
             dma((count,)),

time: 28.3 us -> 26.8 us (0.947)
  Pallas kernels: 27.5 us -> 26 us
    pallas_call x1, Pallas kernels: 27.5 us -> 26 us  [body(): pl.pallas_call(functools.partial(kernel, secs, strips), out_shape=jax.Sha...]
where the time goes in v4:
time: 26.8 us; the launch traced here: 26.6 us
  Pallas kernels  26 us (97%)
  other arithmetic  0.61 us (2%)
    pallas_call x1, Pallas kernels, body(): pl.pallas_call(functools.partial(kernel, secs, strips), out_shape=jax.Sha...  26 us
    add x1, other arithmetic, body(): return state + delta.reshape(state.shape)  0.61 us

profile of v4, /device:TPU:19, one launch (start us, length us, event | category | flops | bytes accessed | tf_op | source)
XLA Modules:
  0.0 26.6 jit_solution(6252601177280554117)
XLA Ops:
  0.0 0.0 copy-start
  0.0 26.0 %shard_map.82 = f32[24,1,128]{2,1,0:T(1,128)S(1)} custom-call(bf16[1,12,128,128]{3,2,1,0:T(8,128)(2,1)} %feat.1, s32[4]{0:T(128)} %offsets.1, bf16[3,3,162,128]{3,2,1,0:T(8,128)(2,1)} %w_one.1, f32[1,128]{1,0:T(1,128)} %bitcast.6, bf16[3,3,128,128]{3,2,1,0:T(8,128)(2,1)} %w_two.1, f32[1,128]{1,0:T(1,128)} %bitcast.7, bf16[3,3,2,128]{3,2,1,0:T(2,128)(2,1)} %bitcast.5), custom_call_target="tpu_custom_call" | custom-call | tf_op jit(solution)/shard_map/pallas_call | solution.py:392
  26.0 0.0 copy-done
  26.0 0.6 %add.3 = f32[2,1,12,128]{3,1,2,0:T(1,128)} add(f32[2,1,12,128]{3,1,2,0:T(1,128)S(1)} %copy-done, f32[2,1,12,128]{3,1,2,0:T(1,128)S(1)} %bitcast.4) | non-fusion elementwise | flops 3072 | bytes 36864 | tf_op jit(solution)/shard_map/add | solution.py:425
Async XLA Ops:
  0.0 26.0 %copy-start = (f32[2,1,12,128]{3,1,2,0:T(1,128)S(1)}, f32[2,1,12,128]{3,1,2,0:T(1,128)}, u32[]{:S(2)}) copy-start(f32[2,1,12,128]{3,1,2,0:T(1,128)} %param.10) | copy-start | bytes 36868

commit v5 on v4

--- a/solution.py
+++ b/solution.py
@@ -54,7 +54,11 @@
                 ready.append((at - EDGE) // PAIR)
         tasks.setdefault(max(ready), []).append(w // QUAD + 1)
     stages = max(max(tasks) + 1, count)
-    width = max(len(found) for found in tasks.values())
+    width = 2
+    for found in tasks.values():
+        found.sort(key=lambda task: min(task - 1, (rows + 2 * EDGE) // QUAD - task))
+    spill = max(len(found) for found in tasks.values())
+    assert spill <= width and rows % QUAD == 0
     return [[(tasks.get(i, []) + [0] * width)[q] for i in range(stages)] for q in range(width)]
 
 
@@ -224,38 +228,50 @@
     def shift_of(s):
         return jnp.where(s == 0, shifts[0], shifts[1])
 
-    def meet(s, w):
+    def full(s, w):
         there = turned(s, w)
-        place = (offset - TAPS * w) & (cols - 1)
         here = mine[pl.ds(w + LEFT - SPAN - 1 - shift_of(s), SPAN + PAIR)]
         tiles = [product(here[v * PAIR:v * PAIR + SPAN], there[v * PAIR:(v + 1) * PAIR]) for v in range(2)]
-        for j in range(SPAN + PAIR):
-            us = [u for u in range(QUAD) if 0 <= TAPS - 1 - j + u < TAPS]
-            kept = met[s, w + j]
-            found = kept
-            for u in reversed(us):
-                r = j - u // PAIR * PAIR
-                one = tiles[u // PAIR][r * cols:(r + 1) * cols, u % PAIR * cols:(u % PAIR + 1) * cols]
-                found = jnp.where(place < TAPS * (u + 1), one, found)
-            if us[0] > 0:
-                found = jnp.where(place < TAPS * us[0], kept, found)
-            met[s, w + j] = found
-
-    def meet_edge(s, w):
+
+        def keep():
+            place = (offset - TAPS * w) & (cols - 1)
+            for j in range(SPAN + PAIR):
+                us = [u for u in range(QUAD) if 0 <= TAPS - 1 - j + u < TAPS]
+                kept = met[s, w + j]
+                found = kept
+                for u in reversed(us):
+                    r = j - u // PAIR * PAIR
+                    one = tiles[u // PAIR][r * cols:(r + 1) * cols, u % PAIR * cols:(u % PAIR + 1) * cols]
+                    found = jnp.where(place < TAPS * (u + 1), one, found)
+                if us[0] > 0:
+                    found = jnp.where(place < TAPS * us[0], kept, found)
+                met[s, w + j] = found
+
+        return keep
+
+    def edge(s, w):
         there = turned(s, w)
-        place = (offset - TAPS * w) & (cols - 1)
         begin = jnp.where(w <= QUAD, SPAN + PAIR - SHORT, 0)
         here = mine[pl.ds(w + begin + LEFT - SPAN - 1 - shift_of(s), SHORT)]
         tiles = [product(here, there[v * PAIR:(v + 1) * PAIR]) for v in range(2)]
-        for r in range(SHORT):
-            j = begin + r
-            low, high = TAPS * jnp.maximum(j - TAPS + 1, 0), TAPS * jnp.minimum(j + 1, QUAD)
-            kept = met[s, w + j]
-            found = tiles[1][r * cols:(r + 1) * cols, cols:]
-            for u in reversed(range(QUAD - 1)):
-                one = tiles[u // PAIR][r * cols:(r + 1) * cols, u % PAIR * cols:(u % PAIR + 1) * cols]
-                found = jnp.where(place < TAPS * (u + 1), one, found)
-            met[s, w + j] = jnp.where((place >= low) & (place < high), found, kept)
+
+        def keep():
+            place = (offset - TAPS * w) & (cols - 1)
+            for r in range(SHORT):
+                j = begin + r
+                low, high = TAPS * jnp.maximum(j - TAPS + 1, 0), TAPS * jnp.minimum(j + 1, QUAD)
+                kept = met[s, w + j]
+                found = tiles[1][r * cols:(r + 1) * cols, cols:]
+                for u in reversed(range(QUAD - 1)):
+                    one = tiles[u // PAIR][r * cols:(r + 1) * cols, u % PAIR * cols:(u % PAIR + 1) * cols]
+                    found = jnp.where(place < TAPS * (u + 1), one, found)
+                met[s, w + j] = jnp.where((place >= low) & (place < high), found, kept)
+
+        return keep
+
+    def meet(*steps):
+        for keep in [act(s, w) for act, s, w in steps]:
+            keep()
 
     def gather(s, e):
         index = (source + TAPS * (e + STEP + shifts[s])) & (cols - 1)
@@ -265,11 +281,11 @@
 
     def gather_some(s, start, end):
         def some(g, carry):
-            for i in range(PAIR):
-                gather(s, start + g * PAIR + i)
+            for i in range(6):
+                gather(s, start + g * 6 + i)
             return carry
 
-        lax.fori_loop(0, (end - start) // PAIR, some, 0)
+        lax.fori_loop(0, (end - start) // 6, some, 0)
 
     def halo(s, at):
         k_beyond = (EDGE - PAIR - at) // PAIR
@@ -282,6 +298,7 @@
 
     table = plan(rows)
     stages, width = len(table[0]), len(table)
+    lone_full = any(QUAD < QUAD * (a - 1) < rows + EDGE + PAIR for a, b in zip(*table) if a > 0 and b == 0)
     codes = [sum(v << (BITS * i) for i, v in enumerate(line)) for line in table]
 
     def step(n, carry):
@@ -305,20 +322,27 @@
         def _():
             tasks = [lax.shift_right_logical(jnp.int32(code), BITS * t) & (2 ** BITS - 1) for code in codes]
 
-            def work(q, carry):
-                task = tasks[0]
-                for i in range(1, width):
-                    task = jnp.where(q == i, tasks[i], task)
-                w = QUAD * (task - 1)
-                halo(s, w)
-                halo(s, w + PAIR)
-                edge = (w <= QUAD) | (w >= rows + EDGE + PAIR)
-                at = jnp.where(core == 0, w, rows + 2 * EDGE - QUAD - w)
-                when(edge, lambda: meet_edge(s, at))
-                when(jnp.logical_not(edge), lambda: meet(s, at))
-                return carry
-
-            lax.fori_loop(0, sum((task > 0).astype(jnp.int32) for task in tasks), work, 0)
+            ws = [QUAD * (task - 1) for task in tasks]
+            ats = [jnp.where(core == 0, w, rows + 2 * EDGE - QUAD - w) for w in ws]
+            short = [(w <= QUAD) | (w >= rows + EDGE + PAIR) for w in ws]
+            has_two = tasks[1] > 0
+
+            @pl.when(tasks[0] > 0)
+            def _():
+                halo(s, ws[0])
+                halo(s, ws[0] + PAIR)
+
+            @pl.when(has_two)
+            def _():
+                halo(s, ws[1])
+                halo(s, ws[1] + PAIR)
+
+            alone = (tasks[0] > 0) & jnp.logical_not(has_two)
+            when(alone & short[0], lambda: meet((edge, s, ats[0])))
+            if lone_full:
+                when(alone & jnp.logical_not(short[0]), lambda: meet((full, s, ats[0])))
+            when(has_two & short[0], lambda: meet((edge, s, ats[0]), (full, s, ats[1])))
+            when(has_two & jnp.logical_not(short[0]), lambda: meet((full, s, ats[0]), (full, s, ats[1])))
 
         when((s == 0) & (j == stages + 1), lambda: gather_some(0, 0, rows + 2 * STEP))
         return carry
@@ -326,9 +350,10 @@
     lax.fori_loop(0, (stages + RELAYED + LATER) * 2, step, 0)
 
     group = group_of(rows + 4)
-    gather_some(1, 0, group + PAIR)
+    ready = pl.cdiv(group + PAIR, 6) * 6
+    gather_some(1, 0, ready)
     for base in range(0, rows + 4, group):
-        for e in range(base + group + PAIR, min(base + 2 * group + PAIR, rows + 2 * STEP)):
+        for e in range(max(base + group + PAIR, ready), min(base + 2 * group + PAIR, rows + 2 * STEP)):
             gather(1, e)
         convolve((corr.at[0], corr.at[1]), main_one, rest_one, bias_one, hid_one, base, group)
 

time: 26.8 us -> 25.5 us (0.951)
  Pallas kernels: 26 us -> 24.8 us
    pallas_call x1, Pallas kernels: 26 us -> 24.8 us  [body(): pl.pallas_call(functools.partial(kernel, secs, strips), out_shape=jax.Sha...]
where the time goes in v5:
time: 25.5 us; the launch traced here: 25.4 us
  Pallas kernels  24.8 us (97%)
  other arithmetic  0.61 us (2%)
    pallas_call x1, Pallas kernels, body(): pl.pallas_call(functools.partial(kernel, secs, strips), out_shape=jax.Sha...  24.8 us
    add x1, other arithmetic, body(): return state + delta.reshape(state.shape)  0.61 us

profile of v5, /device:TPU:19, one launch (start us, length us, event | category | flops | bytes accessed | tf_op | source)
XLA Modules:
  0.0 25.4 jit_solution(10984031744168747174)
XLA Ops:
  0.0 0.0 copy-start
  0.0 24.8 %shard_map.82 = f32[24,1,128]{2,1,0:T(1,128)S(1)} custom-call(bf16[1,12,128,128]{3,2,1,0:T(8,128)(2,1)} %feat.1, s32[4]{0:T(128)} %offsets.1, bf16[3,3,162,128]{3,2,1,0:T(8,128)(2,1)} %w_one.1, f32[1,128]{1,0:T(1,128)} %bitcast.6, bf16[3,3,128,128]{3,2,1,0:T(8,128)(2,1)} %w_two.1, f32[1,128]{1,0:T(1,128)} %bitcast.7, bf16[3,3,2,128]{3,2,1,0:T(2,128)(2,1)} %bitcast.5), custom_call_target="tpu_custom_call" | custom-call | tf_op jit(solution)/shard_map/pallas_call | solution.py:417
  24.8 0.0 copy-done
  24.8 0.6 %add.3 = f32[2,1,12,128]{3,1,2,0:T(1,128)} add(f32[2,1,12,128]{3,1,2,0:T(1,128)S(1)} %copy-done, f32[2,1,12,128]{3,1,2,0:T(1,128)S(1)} %bitcast.4) | non-fusion elementwise | flops 3072 | bytes 36864 | tf_op jit(solution)/shard_map/add | solution.py:450
Async XLA Ops:
  0.0 24.8 %copy-start = (f32[2,1,12,128]{3,1,2,0:T(1,128)S(1)}, f32[2,1,12,128]{3,1,2,0:T(1,128)}, u32[]{:S(2)}) copy-start(f32[2,1,12,128]{3,1,2,0:T(1,128)} %param.10) | copy-start | bytes 36868

commit v6 on v5

--- a/solution.py
+++ b/solution.py
@@ -16,17 +16,18 @@
 EDGE = SIDE + 1
 HALO = EDGE // PAIR
 QUAD = 2 * PAIR
-RELAYED = 2
-LATER = 1
+RELAYED = 3
+LATER = 0
 SHORT = 7
+BLOCK = 6
 BITS = 4
 HBM = pl.BlockSpec(memory_space=pltpu.HBM)
 VMEM = pl.BlockSpec(memory_space=pltpu.VMEM)
 MESH = pl.DeviceIdType.MESH
 
 
-def group_of(rows):
-    return max(g for g in range(2, 15, 2) if rows % g == 0)
+def group_of(rows, most):
+    return max(g for g in range(2, most + 1, 2) if rows % g == 0)
 
 
 def when(cond, act):
@@ -62,7 +63,7 @@
     return [[(tasks.get(i, []) + [0] * width)[q] for i in range(stages)] for q in range(width)]
 
 
-def convolve(sources, weight, tail, bias, target, base, group):
+def convolve(sources, weight, tail, bias, target, base, group, inside):
     cols, width = target.shape[1:]
     at_col = lax.broadcasted_iota(jnp.int32, (cols, width), 0)
 
@@ -79,7 +80,11 @@
         before = jnp.where(at_col == 0, 0.0, pltpu.roll(one[:, :width], 1, 0))
         after = jnp.where(at_col == cols - 1, 0.0, pltpu.roll(other, cols - 1, 0))
         total = one[:, width:2 * width] + before + after + bias[...]
-        target[base + i] = jnp.maximum(total, 0.0).astype(target.dtype)
+        total = jnp.maximum(total, 0.0)
+        known = inside(base + i)
+        if known is not None:
+            total = jnp.where(known, total, 0.0)
+        target[base + i] = total.astype(target.dtype)
 
 
 def kernel(secs, strips, feat, offsets, w_one, b_one, w_two, b_two, w_three, out,
@@ -281,11 +286,11 @@
 
     def gather_some(s, start, end):
         def some(g, carry):
-            for i in range(6):
-                gather(s, start + g * 6 + i)
+            for i in range(BLOCK):
+                gather(s, start + g * BLOCK + i)
             return carry
 
-        lax.fori_loop(0, (end - start) // 6, some, 0)
+        lax.fori_loop(0, (end - start) // BLOCK, some, 0)
 
     def halo(s, at):
         k_beyond = (EDGE - PAIR - at) // PAIR
@@ -344,38 +349,29 @@
             when(has_two & short[0], lambda: meet((edge, s, ats[0]), (full, s, ats[1])))
             when(has_two & jnp.logical_not(short[0]), lambda: meet((full, s, ats[0]), (full, s, ats[1])))
 
-        when((s == 0) & (j == stages + 1), lambda: gather_some(0, 0, rows + 2 * STEP))
+        when((s == 0) & (j == stages + 2), lambda: gather_some(0, 0, rows + 2 * STEP))
         return carry
 
     lax.fori_loop(0, (stages + RELAYED + LATER) * 2, step, 0)
 
-    group = group_of(rows + 4)
-    ready = pl.cdiv(group + PAIR, 6) * 6
+    def within(margin):
+        def known(r):
+            if r < margin:
+                return has_low
+            return has_high if r >= rows + margin else None
+
+        return known
+
+    group = group_of(rows + 4, 4)
+    ready = pl.cdiv(group + PAIR, BLOCK) * BLOCK
     gather_some(1, 0, ready)
     for base in range(0, rows + 4, group):
         for e in range(max(base + group + PAIR, ready), min(base + 2 * group + PAIR, rows + 2 * STEP)):
             gather(1, e)
-        convolve((corr.at[0], corr.at[1]), main_one, rest_one, bias_one, hid_one, base, group)
-
-    @pl.when(strip == 0)
-    def _():
-        hid_one[0:2] = jnp.zeros((2, cols, hid), hid_one.dtype)
-
-    @pl.when(strip == strips - 1)
-    def _():
-        hid_one[rows + 2:] = jnp.zeros((2, cols, hid), hid_one.dtype)
-
-    group = group_of(rows + 2)
+        convolve((corr.at[0], corr.at[1]), main_one, rest_one, bias_one, hid_one, base, group, within(2))
+    group = group_of(rows + 2, 2)
     for base in range(0, rows + 2, group):
-        convolve((hid_one,), main_two, rest_two, bias_two, hid_two, base, group)
-
-    @pl.when(strip == 0)
-    def _():
-        hid_two[0:1] = jnp.zeros((1, cols, hid), hid_two.dtype)
-
-    @pl.when(strip == strips - 1)
-    def _():
-        hid_two[rows + 1:] = jnp.zeros((1, cols, hid), hid_two.dtype)
+        convolve((hid_one,), main_two, rest_two, bias_two, hid_two, base, group, within(1))
 
     taps = lax.dot_general(
         thirds[...].astype(hid_two.dtype), hid_two[...].reshape((rows + 2) * cols, hid), (((1,), (1,)), ((), ())),

time: 25.5 us -> 24.1 us (0.945)
  Pallas kernels: 24.8 us -> 23.3 us
    pallas_call x1, Pallas kernels: 24.8 us -> 23.3 us  [body(): pl.pallas_call(functools.partial(kernel, secs, strips), out_shape=jax.Sha...]
where the time goes in v6:
time: 24.1 us; the launch traced here: 24 us
  Pallas kernels  23.3 us (97%)
  other arithmetic  0.61 us (3%)
    pallas_call x1, Pallas kernels, body(): pl.pallas_call(functools.partial(kernel, secs, strips), out_shape=jax.Sha...  23.3 us
    add x1, other arithmetic, body(): return state + delta.reshape(state.shape)  0.61 us

profile of v6, /device:TPU:19, one launch (start us, length us, event | category | flops | bytes accessed | tf_op | source)
XLA Modules:
  0.0 24.0 jit_solution(16078481409189864132)
XLA Ops:
  0.0 0.0 copy-start
  0.0 23.3 %shard_map.82 = f32[24,1,128]{2,1,0:T(1,128)S(1)} custom-call(bf16[1,12,128,128]{3,2,1,0:T(8,128)(2,1)} %feat.1, s32[4]{0:T(128)} %offsets.1, bf16[3,3,162,128]{3,2,1,0:T(8,128)(2,1)} %w_one.1, f32[1,128]{1,0:T(1,128)} %bitcast.6, bf16[3,3,128,128]{3,2,1,0:T(8,128)(2,1)} %w_two.1, f32[1,128]{1,0:T(1,128)} %bitcast.7, bf16[3,3,2,128]{3,2,1,0:T(2,128)(2,1)} %bitcast.5), custom_call_target="tpu_custom_call" | custom-call | tf_op jit(solution)/shard_map/pallas_call | solution.py:413
  23.3 0.0 copy-done
  23.3 0.6 %add.3 = f32[2,1,12,128]{3,1,2,0:T(1,128)} add(f32[2,1,12,128]{3,1,2,0:T(1,128)S(1)} %copy-done, f32[2,1,12,128]{3,1,2,0:T(1,128)S(1)} %bitcast.4) | non-fusion elementwise | flops 3072 | bytes 36864 | tf_op jit(solution)/shard_map/add | solution.py:446
Async XLA Ops:
  0.0 23.3 %copy-start = (f32[2,1,12,128]{3,1,2,0:T(1,128)S(1)}, f32[2,1,12,128]{3,1,2,0:T(1,128)}, u32[]{:S(2)}) copy-start(f32[2,1,12,128]{3,1,2,0:T(1,128)} %param.10) | copy-start | bytes 36868

commit v7 on v6

--- a/solution.py
+++ b/solution.py
@@ -362,7 +362,7 @@
 
         return known
 
-    group = group_of(rows + 4, 4)
+    group = group_of(rows + 4, 2)
     ready = pl.cdiv(group + PAIR, BLOCK) * BLOCK
     gather_some(1, 0, ready)
     for base in range(0, rows + 4, group):

time: 24.1 us -> 24.1 us (level)
  no operation moved by 1% of the time
where the time goes in v7:
time: 24.1 us; the launch traced here: 23.9 us
  Pallas kernels  23.3 us (97%)
  other arithmetic  0.61 us (3%)
    pallas_call x1, Pallas kernels, body(): pl.pallas_call(functools.partial(kernel, secs, strips), out_shape=jax.Sha...  23.3 us
    add x1, other arithmetic, body(): return state + delta.reshape(state.shape)  0.61 us

profile of v7, /device:TPU:19, one launch (start us, length us, event | category | flops | bytes accessed | tf_op | source)
XLA Modules:
  0.0 23.9 jit_solution(16461462609980773302)
XLA Ops:
  0.0 0.0 copy-start
  0.0 23.3 %shard_map.82 = f32[24,1,128]{2,1,0:T(1,128)S(1)} custom-call(bf16[1,12,128,128]{3,2,1,0:T(8,128)(2,1)} %feat.1, s32[4]{0:T(128)} %offsets.1, bf16[3,3,162,128]{3,2,1,0:T(8,128)(2,1)} %w_one.1, f32[1,128]{1,0:T(1,128)} %bitcast.6, bf16[3,3,128,128]{3,2,1,0:T(8,128)(2,1)} %w_two.1, f32[1,128]{1,0:T(1,128)} %bitcast.7, bf16[3,3,2,128]{3,2,1,0:T(2,128)(2,1)} %bitcast.5), custom_call_target="tpu_custom_call" | custom-call | tf_op jit(solution)/shard_map/pallas_call | solution.py:413
  23.3 0.0 copy-done
  23.3 0.6 %add.3 = f32[2,1,12,128]{3,1,2,0:T(1,128)} add(f32[2,1,12,128]{3,1,2,0:T(1,128)S(1)} %copy-done, f32[2,1,12,128]{3,1,2,0:T(1,128)S(1)} %bitcast.4) | non-fusion elementwise | flops 3072 | bytes 36864 | tf_op jit(solution)/shard_map/add | solution.py:446
Async XLA Ops:
  0.0 23.3 %copy-start = (f32[2,1,12,128]{3,1,2,0:T(1,128)S(1)}, f32[2,1,12,128]{3,1,2,0:T(1,128)}, u32[]{:S(2)}) copy-start(f32[2,1,12,128]{3,1,2,0:T(1,128)} %param.10) | copy-start | bytes 36868
